TPU v7x, 32 devices: a whole 2x2x4 slice. The times are simulated.
32 devices in a mesh: seq: 2 (over core), hid: 16 (over z, y, x).
Axes of the slice: x: 2, y: 2, z: 4, core: 2. Of those that a mesh axis runs over, the one named last changes fastest.
Arguments:
- inputs: bfloat16 [2, 768, 2048], P('seq', 'hid'), may hold values from -6 to 6
- cotangent: bfloat16 [2, 768, 2048], P('seq', 'hid'), may hold values from -6 to 6
- lengths: int32 [12], replicated, may hold values from 1 to 1024, 1536 in all
- first_gain: float32 [2048], replicated, may hold values from 0.25 to 1.75
- q_weight: bfloat16 [2048, 2048], P(('seq', 'hid')), may hold values from -0.125 to 0.125
- f_weight: bfloat16 [2048, 2048], P(('seq', 'hid')), may hold values from -0.125 to 0.125
- i_weight: bfloat16 [2048, 2048], P(('seq', 'hid')), may hold values from -0.125 to 0.125
- o_weight: bfloat16 [2048, 2048], P(('seq', 'hid')), may hold values from -0.125 to 0.125
- group_gain: float32 [128], replicated, may hold values from 0.25 to 1.75
- gap_log: float32 [2048], replicated, may hold values from -11.5 to -3.5
- second_gain: float32 [2048], replicated, may hold values from 0.25 to 1.75
- gate_weight: bfloat16 [2048, 5632], P(('seq', 'hid')), may hold values from -0.125 to 0.125
- up_weight: bfloat16 [2048, 5632], P(('seq', 'hid')), may hold values from -0.125 to 0.125
- down_weight: bfloat16 [2048, 5632], P(('seq', 'hid')), may hold values from -0.078125 to 0.078125
Outputs:
- output: bfloat16 [2, 768, 2048], P('seq', 'hid')
- input_grad: float32 [2, 768, 2048], P('seq', 'hid')
- first_grad: float32 [2048], replicated
- q_grad: float32 [2048, 2048], P(('seq', 'hid'))
- f_grad: float32 [2048, 2048], P(('seq', 'hid'))
- i_grad: float32 [2048, 2048], P(('seq', 'hid'))
- o_grad: float32 [2048, 2048], P(('seq', 'hid'))
- group_grad: float32 [128], replicated
- gap_grad: float32 [2048], replicated
- second_grad: float32 [2048], replicated
- gate_grad: float32 [2048, 5632], P(('seq', 'hid'))
- up_grad: float32 [2048, 5632], P(('seq', 'hid'))
- down_grad: float32 [2048, 5632], P(('seq', 'hid'))
Inputs may be any that keep to these rules, and one draw needn't show every extreme that they name: The 12 documents fill the 1536 positions in order; the lengths sum to 1536 and the largest is exactly 1024.
All inputs are finite; a program needn't handle non-finite values.
Results may differ from a plain program's by a relative error of at most 0.015.
Values may be sent and summed in bfloat16 or wider, within the bound.
A program may use at most 320 MiB of HBM per device.

v0:
```python
import jax
import jax.numpy as jnp
from jax import lax
from jax.sharding import PartitionSpec as P

H = 16
SPAN = 128


EPS = 1e-06
HIGH_PRECISION = lax.Precision.HIGHEST


def from_behind(block, axis, distance):
    devices = range(lax.axis_size(axis))
    route = [(i - distance, i) for i in devices if i - distance in devices]
    return lax.ppermute(block, axis, route)


def normed(entries, gain_vec):
    factor = lax.rsqrt(jnp.mean(entries * entries, axis=-1, keepdims=True) + EPS)
    return entries * factor * gain_vec


def gates(q_part, f_part, gap_piece):
    key_gate = jnp.exp(gap_piece) * jax.nn.sigmoid(-f_part)
    return (jax.nn.silu(q_part), key_gate, jnp.log1p(-key_gate))


def doc_ids(lengths, positions):
    starts = jnp.cumsum(lengths) - lengths
    covered = (starts[None, :] <= positions[:, None]).astype(jnp.int32)
    return jnp.sum(covered, axis=1) - 1


def span_step(memory_state, pieces):
    queries, key_gate, value_rows, log_decay, documents, before = pieces
    cumulative = jnp.cumsum(log_decay, axis=1)
    query_decayed = queries * jnp.exp(cumulative)
    k_grown = key_gate * jnp.exp(-cumulative)
    extent = documents.shape[0]
    row_ids = lax.broadcasted_iota(jnp.int32, (extent, extent), 0)
    col_ids = lax.broadcasted_iota(jnp.int32, (extent, extent), 1)
    same_doc = jnp.logical_and(documents[:, None] == documents[None, :], row_ids >= col_ids).astype(
        jnp.float32
    )
    scores = (
        jnp.einsum("hck,hsk->hcs", query_decayed, k_grown, precision=HIGH_PRECISION)
        * same_doc[None]
    )
    within_block = jnp.einsum("hcs,hsv->hcv", scores, value_rows, precision=HIGH_PRECISION)
    carried_state = (documents == before).astype(jnp.float32)[None, :, None]
    output_rows = within_block + carried_state * jnp.einsum(
        "awn,ani->awi", query_decayed, memory_state, precision=HIGH_PRECISION
    )
    last_cum = cumulative[:, -1:, :]
    keep_mask = (documents == documents[-1]).astype(jnp.float32)[None, :, None]
    tail_key_rows = jnp.exp(last_cum - cumulative) * key_gate * keep_mask
    whole_block = (documents[-1] == before).astype(jnp.float32)
    fresh_state = jnp.einsum("wfx,wfg->wxg", tail_key_rows, value_rows, precision=HIGH_PRECISION)
    memory_state = jnp.exp(last_cum[:, 0, :])[:, :, None] * whole_block * memory_state + fresh_state
    return (memory_state, output_rows)


def recur(queries, key_gate, value_rows, log_decay, documents, before, memory_state):
    head_count, extent, columns = queries.shape
    span_count = extent // SPAN

    def by_span(tensor):
        return jnp.swapaxes(tensor.reshape(head_count, span_count, SPAN, tensor.shape[-1]), 0, 1)

    doc_rows = documents.reshape(span_count, SPAN)
    befores = jnp.concatenate([jnp.reshape(before, (1,)), doc_rows[:-1, -1]])
    memory_state, span_out = lax.scan(
        jax.checkpoint(span_step),
        memory_state,
        (
            by_span(queries),
            by_span(key_gate),
            by_span(value_rows),
            by_span(log_decay),
            doc_rows,
            befores,
        ),
    )
    return (
        jnp.swapaxes(span_out, 0, 1).reshape(head_count, extent, value_rows.shape[-1]),
        memory_state,
    )


def spread_cols(weight, copies):
    row_count = weight.shape[0]
    shaped = weight.reshape(row_count, 1, H, weight.shape[1] // H)
    return jnp.broadcast_to(shaped, (row_count, copies, H, shaped.shape[3])).reshape(
        row_count, copies * weight.shape[1]
    )


def fold_copies(received, copies):
    row_count = received.shape[0]
    return jnp.sum(received.reshape(row_count, copies, received.shape[1] // copies), axis=1)


def fan_rows(local_rows):
    blocks_here, row_count, columns = local_rows.shape
    return jnp.broadcast_to(local_rows[:, None], (blocks_here, H, row_count, columns)).reshape(
        blocks_here * H * row_count, columns
    )


def sum_heads(received, blocks_here):
    total_rows, columns = received.shape
    return jnp.sum(
        received.reshape(blocks_here, H, total_rows // (blocks_here * H), columns), axis=1
    )


def times_t(left_mat, right_mat):
    return lax.dot_general(
        left_mat, right_mat, (((1,), (1,)), ((), ())), preferred_element_type=jnp.float32
    )


def outer_sum(left_mat, right_mat):
    return lax.dot_general(
        left_mat, right_mat, (((0,), (0,)), ((), ())), preferred_element_type=jnp.float32
    )


def outer_high(left_mat, right_mat):
    return lax.dot_general(
        left_mat,
        right_mat,
        (((0,), (0,)), ((), ())),
        precision=HIGH_PRECISION,
        preferred_element_type=jnp.float32,
    )


def body(
    inputs,
    cotangent,
    lengths,
    first_gain,
    q_weight,
    f_weight,
    i_weight,
    o_weight,
    group_gain,
    gap_log,
    second_gain,
    gate_weight,
    up_weight,
    down_weight,
):
    hid_size = lax.axis_size("hid")
    per_seq = hid_size // H
    block_total = lax.axis_size("seq") * per_seq
    hid_place = lax.axis_index("hid")
    head_id = hid_place % H
    block_id = lax.axis_index("seq") * per_seq + hid_place // H
    model = inputs.shape[2]
    head_width = model // H
    block_len = hid_size * inputs.shape[1]
    entries = inputs.astype(jnp.float32)
    q_block, f_block, i_block, o_block, gate_block, up_block, down_block = (
        lax.all_to_all(
            spread_cols(q_weight, block_total),
            ("seq", "hid"),
            split_axis=1,
            concat_axis=0,
            tiled=True,
        ),
        lax.all_to_all(
            spread_cols(f_weight, block_total),
            ("seq", "hid"),
            split_axis=1,
            concat_axis=0,
            tiled=True,
        ),
        lax.all_to_all(
            spread_cols(i_weight, block_total),
            ("seq", "hid"),
            split_axis=1,
            concat_axis=0,
            tiled=True,
        ),
        lax.all_to_all(
            spread_cols(o_weight, block_total),
            ("seq", "hid"),
            split_axis=1,
            concat_axis=0,
            tiled=True,
        ),
        lax.all_to_all(
            spread_cols(gate_weight, block_total),
            ("seq", "hid"),
            split_axis=1,
            concat_axis=0,
            tiled=True,
        ),
        lax.all_to_all(
            spread_cols(up_weight, block_total),
            ("seq", "hid"),
            split_axis=1,
            concat_axis=0,
            tiled=True,
        ),
        lax.all_to_all(
            spread_cols(down_weight, block_total),
            ("seq", "hid"),
            split_axis=1,
            concat_axis=0,
            tiled=True,
        ),
    )
    positions = block_id * block_len + lax.iota(jnp.int32, block_len)
    documents = doc_ids(lengths, positions)
    before = doc_ids(lengths, jnp.reshape(block_id * block_len - 1, (1,)))[0]
    first_norm, first_back = jax.vjp(normed, entries, first_gain)
    first_low = first_norm.astype(jnp.bfloat16)
    first_rows = lax.all_to_all(fan_rows(first_low), "hid", split_axis=0, concat_axis=0, tiled=True)
    q_lin = jnp.dot(first_rows, q_block, preferred_element_type=jnp.float32)
    f_lin = jnp.dot(first_rows, f_block, preferred_element_type=jnp.float32)
    i_lin = jnp.dot(first_rows, i_block, preferred_element_type=jnp.float32)
    gap_part = lax.dynamic_slice_in_dim(gap_log, head_id * head_width, head_width)
    queries, key_gate, log_decay = gates(q_lin, f_lin, gap_part)
    cumulative = jnp.cumsum(log_decay, axis=0)
    last_cum = cumulative[-1]
    tail_key_rows = (
        jnp.exp(last_cum[None, :] - cumulative)
        * key_gate
        * (documents == documents[-1]).astype(jnp.float32)[:, None]
    )
    local_state = outer_high(tail_key_rows, i_lin)
    decay = jnp.exp(last_cum) * (documents[-1] == before).astype(jnp.float32)
    state_in = jnp.zeros_like(local_state)
    for number in range(block_total - 1):
        state_out = decay[:, None] * state_in + local_state
        state_in = from_behind(state_out.astype(jnp.bfloat16), ("seq", "hid"), H).astype(
            state_out.dtype
        )

    def core(q_part, f_part, i_part, gap_piece):
        queries_in, keys_in, logs_in = gates(q_part, f_part, gap_piece)
        mixed_all, memory_state = recur(
            queries_in[None],
            keys_in[None],
            i_part[None],
            logs_in[None],
            documents,
            before,
            state_in[None],
        )
        return (mixed_all[0], memory_state[0])

    (mixed_out, _), core_back = jax.vjp(core, q_lin, f_lin, i_lin, gap_part)
    head_normed, norm_back = jax.vjp(normed, mixed_out, group_gain)
    head_low = head_normed.astype(jnp.bfloat16)
    mix_out = sum_heads(
        lax.all_to_all(
            times_t(head_low, o_block).astype(jnp.bfloat16),
            "hid",
            split_axis=0,
            concat_axis=0,
            tiled=True,
        ).astype(jnp.float32),
        per_seq,
    )
    middle = entries + mix_out
    second_norm, second_back = jax.vjp(normed, middle, second_gain)
    second_low = second_norm.astype(jnp.bfloat16)
    second_rows, cot_rows = (
        lax.all_to_all(fan_rows(second_low), "hid", split_axis=0, concat_axis=0, tiled=True),
        lax.all_to_all(fan_rows(cotangent), "hid", split_axis=0, concat_axis=0, tiled=True),
    )
    gate_lin = jnp.dot(second_rows, gate_block, preferred_element_type=jnp.float32)
    up_lin = jnp.dot(second_rows, up_block, preferred_element_type=jnp.float32)
    hidden = (jax.nn.silu(gate_lin) * up_lin).astype(jnp.bfloat16)
    glu_out = sum_heads(
        lax.all_to_all(
            times_t(hidden, down_block).astype(jnp.bfloat16),
            "hid",
            split_axis=0,
            concat_axis=0,
            tiled=True,
        ).astype(jnp.float32),
        per_seq,
    )
    output = (middle + glu_out).astype(jnp.bfloat16)
    down_part = outer_sum(cot_rows, hidden)
    hidden_grad = jnp.dot(cot_rows, down_block, preferred_element_type=jnp.float32)
    gate_sig = jax.nn.sigmoid(gate_lin)
    gate_low = (hidden_grad * up_lin * gate_sig * (1.0 + gate_lin * (1.0 - gate_sig))).astype(
        jnp.bfloat16
    )
    up_low = (hidden_grad * gate_lin * gate_sig).astype(jnp.bfloat16)
    gate_part = outer_sum(second_rows, gate_low)
    up_part = outer_sum(second_rows, up_low)
    second_sum = lax.all_to_all(
        (times_t(gate_low, gate_block) + times_t(up_low, up_block)).astype(jnp.bfloat16),
        "hid",
        split_axis=0,
        concat_axis=0,
        tiled=True,
    ).astype(jnp.float32)
    middle_part, second_part = second_back(sum_heads(second_sum, per_seq))
    middle_grad = cotangent.astype(jnp.float32) + middle_part
    mix_grad = middle_grad.astype(jnp.bfloat16)
    mix_rows = lax.all_to_all(fan_rows(mix_grad), "hid", split_axis=0, concat_axis=0, tiled=True)
    normed_grad = jnp.dot(mix_rows, o_block, preferred_element_type=jnp.float32)
    o_part = outer_sum(mix_rows, head_low)
    mixed_grad, group_part = norm_back(normed_grad)
    carried_state = (documents == before).astype(jnp.float32)[:, None]
    grad_local = outer_high(queries * jnp.exp(cumulative) * carried_state, mixed_grad)
    state_grad = jnp.zeros_like(grad_local)
    for number in range(block_total - 1):
        grad_in = decay[:, None] * state_grad + grad_local
        state_grad = from_behind(grad_in.astype(jnp.bfloat16), ("seq", "hid"), -H).astype(
            grad_in.dtype
        )
    q_grad_lin, f_grad_lin, i_grad_lin, gap_piece_grad = core_back((mixed_grad, state_grad))
    q_low = q_grad_lin.astype(jnp.bfloat16)
    f_low = f_grad_lin.astype(jnp.bfloat16)
    i_low = i_grad_lin.astype(jnp.bfloat16)
    q_part = outer_sum(first_rows, q_low)
    f_part = outer_sum(first_rows, f_low)
    i_part = outer_sum(first_rows, i_low)
    first_sum = lax.all_to_all(
        (times_t(q_low, q_block) + times_t(f_low, f_block) + times_t(i_low, i_block)).astype(
            jnp.bfloat16
        ),
        "hid",
        split_axis=0,
        concat_axis=0,
        tiled=True,
    ).astype(jnp.float32)
    entry_part, first_part = first_back(sum_heads(first_sum, per_seq))
    input_grad = middle_grad + entry_part
    q_back, f_back, i_back, o_back, gate_back, up_back, down_back = (
        lax.all_to_all(
            q_part.astype(jnp.bfloat16), ("seq", "hid"), split_axis=0, concat_axis=1, tiled=True
        ).astype(q_part.dtype),
        lax.all_to_all(
            f_part.astype(jnp.bfloat16), ("seq", "hid"), split_axis=0, concat_axis=1, tiled=True
        ).astype(f_part.dtype),
        lax.all_to_all(
            i_part.astype(jnp.bfloat16), ("seq", "hid"), split_axis=0, concat_axis=1, tiled=True
        ).astype(i_part.dtype),
        lax.all_to_all(
            o_part.astype(jnp.bfloat16), ("seq", "hid"), split_axis=0, concat_axis=1, tiled=True
        ).astype(o_part.dtype),
        lax.all_to_all(
            gate_part.astype(jnp.bfloat16), ("seq", "hid"), split_axis=0, concat_axis=1, tiled=True
        ).astype(gate_part.dtype),
        lax.all_to_all(
            up_part.astype(jnp.bfloat16), ("seq", "hid"), split_axis=0, concat_axis=1, tiled=True
        ).astype(up_part.dtype),
        lax.all_to_all(
            down_part.astype(jnp.bfloat16), ("seq", "hid"), split_axis=0, concat_axis=1, tiled=True
        ).astype(down_part.dtype),
    )
    o_grad = fold_copies(o_back, block_total)
    head_pick = (lax.iota(jnp.int32, H) == head_id).astype(jnp.float32)
    gap_full = (head_pick[:, None] * gap_piece_grad[None, :]).reshape(model)
    first_grad, second_grad, group_grad, gap_grad = lax.psum(
        (first_part, second_part, group_part, gap_full), ("seq", "hid")
    )
    return (
        output,
        input_grad,
        first_grad,
        fold_copies(q_back, block_total),
        fold_copies(f_back, block_total),
        fold_copies(i_back, block_total),
        o_grad,
        group_grad,
        gap_grad,
        second_grad,
        fold_copies(gate_back, block_total),
        fold_copies(up_back, block_total),
        fold_copies(down_back, block_total),
    )


def solution(mesh):
    placed = (
        P("seq", "hid", None),
        P("seq", "hid", None),
        P(),
        P(),
        P(("seq", "hid"), None),
        P(("seq", "hid"), None),
        P(("seq", "hid"), None),
        P(("seq", "hid"), None),
        P(),
        P(),
        P(),
        P(("seq", "hid"), None),
        P(("seq", "hid"), None),
        P(("seq", "hid"), None),
    )
    return jax.shard_map(
        body,
        mesh=mesh,
        in_specs=placed,
        out_specs=(
            P("seq", "hid", None),
            P("seq", "hid", None),
            P(),
            P(("seq", "hid"), None),
            P(("seq", "hid"), None),
            P(("seq", "hid"), None),
            P(("seq", "hid"), None),
            P(),
            P(),
            P(),
            P(("seq", "hid"), None),
            P(("seq", "hid"), None),
            P(("seq", "hid"), None),
        ),
        check_vma=False,
    )
```

profile of v0, /device:TPU:2, one launch (start us, length us, event | category | flops | bytes accessed | tf_op | source)
XLA Modules:
  0.0 1292.8 jit_solution(7225538701237348739)
XLA Ops:
  9.8 14.0 %all-to-all-done.3 = bf16[64,32,128]{2,0,1:T(8,128)(2,1)S(1)} async-done(((bf16[64,32,128]{2,0,1:T(8,128)(2,1)}), bf16[64,32,128]{2,0,1:T(8,128)(2,1)S(1)}, u32[]{:S(2)}, u32[]{:S(2)}) %all-to-all-start.3) | async-done | bytes 524320 | tf_op jit(solution)/shard_map/all_to_all | solution.py:168
  29.2 15.1 %all-to-all-done.1 = bf16[64,32,128]{2,0,1:T(8,128)(2,1)S(1)} async-done(((bf16[64,32,128]{2,0,1:T(8,128)(2,1)}), bf16[64,32,128]{2,0,1:T(8,128)(2,1)S(1)}, u32[]{:S(2)}, u32[]{:S(2)}) %all-to-all-start.1) | async-done | bytes 524320 | tf_op jit(solution)/shard_map/all_to_all | solution.py:175
  49.6 15.1 %all-to-all-done.2 = bf16[64,32,128]{2,0,1:T(8,128)(2,1)S(1)} async-done(((bf16[64,32,128]{2,0,1:T(8,128)(2,1)}), bf16[64,32,128]{2,0,1:T(8,128)(2,1)S(1)}, u32[]{:S(2)}, u32[]{:S(2)}) %all-to-all-start.2) | async-done | bytes 524320 | tf_op jit(solution)/shard_map/all_to_all | solution.py:182
  70.3 14.8 %all-to-all-done.4 = bf16[64,32,128]{2,0,1:T(8,128)(2,1)S(1)} async-done(((bf16[64,32,128]{2,0,1:T(8,128)(2,1)}), bf16[64,32,128]{2,0,1:T(8,128)(2,1)S(1)}, u32[]{:S(2)}, u32[]{:S(2)}) %all-to-all-start.4) | async-done | bytes 524320 | tf_op jit(solution)/shard_map/all_to_all | solution.py:189
  102.9 50.7 %all-to-all-done = bf16[16,48,2048]{2,1,0:T(8,128)(2,1)S(1)} async-done(((bf16[16,48,2048]{2,1,0:T(8,128)(2,1)}), bf16[16,48,2048]{2,1,0:T(8,128)(2,1)S(1)}, u32[]{:S(2)}, u32[]{:S(2)}) %all-to-all-start) | async-done | bytes 3145760 | tf_op jit(solution)/shard_map/all_to_all | solution.py:223
  156.2 13.7 %all-to-all-start.7 = ((bf16[64,32,352]{2,0,1:T(8,128)(2,1)}), bf16[64,32,352]{2,0,1:T(8,128)(2,1)}, u32[]{:S(2)}, u32[]{:S(2)}) async-start(bf16[64,32,352]{2,0,1:T(8,128)(2,1)} %bitcast.586), calls=%async_computation.7 | async-start | bytes 3145728 | tf_op jit(solution)/shard_map/all_to_all | solution.py:196
  190.1 16.6 %all-to-all-done.7 = bf16[64,32,352]{2,0,1:T(8,128)(2,1)} async-done(((bf16[64,32,352]{2,0,1:T(8,128)(2,1)}), bf16[64,32,352]{2,0,1:T(8,128)(2,1)}, u32[]{:S(2)}, u32[]{:S(2)}) %all-to-all-start.7) | async-done | bytes 1441824 | tf_op jit(solution)/shard_map/all_to_all | solution.py:196
  209.3 6.4 all-to-all-start.8
  217.2 71.2 %while.38 = (s32[]{:T(128)}, f32[1,128,128]{2,1,0:T(8,128)S(1)}, f32[6,1,128,128]{3,2,1,0:T(8,128)}, f32[6,1,128,128]{3,2,1,0:T(8,128)}, f32[6,1,128,128]{3,2,1,...) while((s32[]{:T(128)}, f32[1,128,128]{2,1,0:T(8,128)S(1)}, ...), condition=%wide.region_8.9_spmd.clone, body=%wide.region_6.8_spmd.clone.sunk | while | flops 102990464 | bytes 1583807 | solution.py:74
  295.2 7.1 all-to-all-start.5
  307.6 56.8 %all-to-all-done.5 = bf16[16,48,2048]{2,1,0:T(8,128)(2,1)} async-done(((bf16[16,48,2048]{2,1,0:T(8,128)(2,1)}), bf16[16,48,2048]{2,1,0:T(8,128)(2,1)}, u32[]{:S(2)}, u32[]{:S(2)}) %all-to-all-start.5) | async-done | bytes 3145760 | tf_op jit(solution)/shard_map/all_to_all | solution.py:262
  366.9 13.8 %all-to-all-start.9 = ((bf16[64,32,352]{2,0,1:T(8,128)(2,1)}), bf16[64,32,352]{2,0,1:T(8,128)(2,1)}, u32[]{:S(2)}, u32[]{:S(2)}) async-start(bf16[64,32,352]{2,0,1:T(8,128)(2,1)} %bitcast.589), calls=%async_computation.9 | async-start | bytes 3145728 | tf_op jit(solution)/shard_map/all_to_all | solution.py:210
  384.3 33.3 %all-to-all-done.9 = bf16[64,32,352]{2,0,1:T(8,128)(2,1)} async-done(((bf16[64,32,352]{2,0,1:T(8,128)(2,1)}), bf16[64,32,352]{2,0,1:T(8,128)(2,1)}, u32[]{:S(2)}, u32[]{:S(2)}) %all-to-all-start.9) | async-done | bytes 1441824 | tf_op jit(solution)/shard_map/all_to_all | solution.py:210
  418.0 76.2 %all_to_all.296 = bf16[16,48,2048]{2,1,0:T(8,128)(2,1)} all-to-all(bf16[16,48,2048]{2,1,0:T(8,128)(2,1)S(1)} %broadcast_in_dim.202), channel_id=1, replica_groups=mesh['seq'=2,'hid'=16] {'hid'}, dimensions={0} | all-to-all | bytes 6291456 | tf_op jit(solution)/shard_map/all_to_all | solution.py:275
  510.6 50.8 %all-to-all-done.11 = bf16[16,48,2048]{2,1,0:T(8,128)(2,1)} async-done(((bf16[16,48,2048]{2,1,0:T(8,128)(2,1)}), bf16[16,48,2048]{2,1,0:T(8,128)(2,1)}, u32[]{:S(2)}, u32[]{:S(2)}) %all-to-all-start.11) | async-done | bytes 3145760 | tf_op jit(solution)/shard_map/all_to_all | solution.py:276
  574.7 13.8 %all-to-all-start.21 = ((bf16[32,64,352]{2,1,0:T(8,128)(2,1)}), bf16[32,64,352]{2,1,0:T(8,128)(2,1)}, u32[]{:S(2)}, u32[]{:S(2)}) async-start(bf16[32,64,352]{2,1,0:T(8,128)(2,1)} %bitcast.590), calls=%async_computation.21 | async-start | bytes 3145728 | tf_op jit(solution)/shard_map/all_to_all | solution.py:360
  595.5 29.9 %all-to-all-done.21 = bf16[32,64,352]{2,1,0:T(8,128)(2,1)} async-done(((bf16[32,64,352]{2,1,0:T(8,128)(2,1)}), bf16[32,64,352]{2,1,0:T(8,128)(2,1)}, u32[]{:S(2)}, u32[]{:S(2)}) %all-to-all-start.21) | async-done | bytes 1441824 | tf_op jit(solution)/shard_map/all_to_all | solution.py:360
  639.6 28.5 %all-to-all-done.19 = bf16[32,64,352]{2,1,0:T(8,128)(2,1)} async-done(((bf16[32,64,352]{2,1,0:T(8,128)(2,1)}), bf16[32,64,352]{2,1,0:T(8,128)(2,1)}, u32[]{:S(2)}, u32[]{:S(2)}) %all-to-all-start.19) | async-done | bytes 1441824 | tf_op jit(solution)/shard_map/all_to_all | solution.py:354
  668.1 7.0 all-to-all-start.12
  682.2 54.4 %all-to-all-done.12 = bf16[16,48,2048]{2,1,0:T(8,128)(2,1)} async-done(((bf16[16,48,2048]{2,1,0:T(8,128)(2,1)}), bf16[16,48,2048]{2,1,0:T(8,128)(2,1)}, u32[]{:S(2)}, u32[]{:S(2)}) %all-to-all-start.12) | async-done | bytes 3145760 | tf_op jit(solution)/shard_map/all_to_all | solution.py:301
  736.5 13.7 %all-to-all-start.20 = ((bf16[32,64,352]{2,1,0:T(8,128)(2,1)}), bf16[32,64,352]{2,1,0:T(8,128)(2,1)}, u32[]{:S(2)}, u32[]{:S(2)}) async-start(bf16[32,64,352]{2,1,0:T(8,128)(2,1)} %bitcast.587), calls=%async_computation.20 | async-start | bytes 3145728 | tf_op jit(solution)/shard_map/all_to_all | solution.py:357
  754.5 32.6 %all-to-all-done.20 = bf16[32,64,352]{2,1,0:T(8,128)(2,1)} async-done(((bf16[32,64,352]{2,1,0:T(8,128)(2,1)}), bf16[32,64,352]{2,1,0:T(8,128)(2,1)}, u32[]{:S(2)}, u32[]{:S(2)}) %all-to-all-start.20) | async-done | bytes 1441824 | tf_op jit(solution)/shard_map/all_to_all | solution.py:357
  790.1 7.0 all-to-all-start.13
  802.3 56.3 %all-to-all-done.13 = bf16[16,48,2048]{2,1,0:T(8,128)(2,1)} async-done(((bf16[16,48,2048]{2,1,0:T(8,128)(2,1)}), bf16[16,48,2048]{2,1,0:T(8,128)(2,1)}, u32[]{:S(2)}, u32[]{:S(2)}) %all-to-all-start.13) | async-done | bytes 3145760 | tf_op jit(solution)/shard_map/all_to_all | solution.py:311
  858.6 15.3 %all-to-all-start.10 = ((bf16[16,48,2048]{2,1,0:T(8,128)(2,1)}), bf16[16,48,2048]{2,1,0:T(8,128)(2,1)}, u32[]{:S(2)}, u32[]{:S(2)}) async-start(bf16[16,48,2048]{2,1,0:T(8,128)(2,1)} %bitcast.597), calls=%async_computation.10 | async-start | bytes 6291456 | tf_op jit(solution)/shard_map/all_to_all | solution.py:282
  884.3 49.3 %all-to-all-done.10 = bf16[16,48,2048]{2,1,0:T(8,128)(2,1)} async-done(((bf16[16,48,2048]{2,1,0:T(8,128)(2,1)}), bf16[16,48,2048]{2,1,0:T(8,128)(2,1)}, u32[]{:S(2)}, u32[]{:S(2)}) %all-to-all-start.10) | async-done | bytes 3145760 | tf_op jit(solution)/shard_map/all_to_all | solution.py:282
  933.5 13.8 %all-to-all-start.18 = ((bf16[32,64,128]{2,1,0:T(8,128)(2,1)}), bf16[32,64,128]{2,1,0:T(8,128)(2,1)}, u32[]{:S(2)}, u32[]{:S(2)}) async-start(bf16[32,64,128]{2,1,0:T(8,128)(2,1)} %bitcast.598), calls=%async_computation.18 | async-start | bytes 1048576 | tf_op jit(solution)/shard_map/all_to_all | solution.py:351
  950.4 135.1 %while.37 = (s32[]{:T(128)}, f32[1,128,128]{1,2,0:T(8,128)S(1)}, f32[6,1,128,128]{3,2,1,0:T(8,128)}, f32[6,1,128,128]{3,2,1,0:T(8,128)}, bf16[6,1,128,128]{3,2,0...) while((s32[]{:T(128)}, f32[1,128,128]{1,2,0:T(8,128)S(1)}, ...), condition=%wide.region_21.22_spmd, body=%wide.region_16.21_spmd.sunk | while | flops 231490304 | bytes 5027615 | solution.py:74
  1098.5 10.7 all-to-all-done.17
  1120.6 8.7 all-to-all-done.16
  1139.6 9.8 all-to-all-done.15
  1250.8 41.8 %all-reduce.1 = (f32[2048]{0:T(1024)}, f32[128]{0:T(128)}, f32[2048]{0:T(1024)}, f32[2048]{0:T(1024)}) all-reduce(f32[2048]{0:T(1024)S(1)} %get-tuple-element.485, f32[128]{0:T(128)S(1)} %copy-done.59, f32[2048]{0:T(1024)S(1)} %multiply_bitcast_fusion, f32[2048]{0:T(1024)S(1)} %copy-done.42), channel_id=1, replica_groups=mesh['seq'=2,'hid'=16] {'seq','hid'}, use_global_device_ids=true, to_apply=%region_25.26 | all-reduce | flops 6272 | bytes 50176 | tf_op jit(solution)/shard_map/psum | solution.py:367
  (528 shorter events, 496.4 us)
Async XLA Ops:
  1.7 47.9 %copy-start.38 = (bf16[64,2048]{1,0:T(8,128)(2,1)S(1)}, bf16[64,2048]{1,0:T(8,128)(2,1)}, u32[]{:S(2)}) copy-start(bf16[64,2048]{1,0:T(8,128)(2,1)} %param.25) | copy-start | bytes 786436
  2.6 21.2 %all-to-all-start.3 = ((bf16[64,32,128]{2,0,1:T(8,128)(2,1)}), bf16[64,32,128]{2,0,1:T(8,128)(2,1)S(1)}, u32[]{:S(2)}, u32[]{:S(2)}) async-start(bf16[64,32,128]{2,0,1:T(8,128)(2,1)} %bitcast.62), calls=%async_computation.3 | async-start | bytes 1048576 | tf_op jit(solution)/shard_map/all_to_all | solution.py:168
  9.7 60.2 %copy-start.10 = (bf16[1,48,2048]{2,1,0:T(8,128)(2,1)S(1)}, bf16[1,48,2048]{2,1,0:T(8,128)(2,1)}, u32[]{:S(2)}) copy-start(bf16[1,48,2048]{2,1,0:T(8,128)(2,1)} %param.18) | copy-start | bytes 589828
  24.7 45.4 %copy-start.40 = (f32[2048]{0:T(1024)S(1)}, f32[2048]{0:T(1024)}, u32[]{:S(2)}) copy-start(f32[2048]{0:T(1024)} %param.21) | copy-start | bytes 24580
  24.7 19.6 %all-to-all-start.1 = ((bf16[64,32,128]{2,0,1:T(8,128)(2,1)}), bf16[64,32,128]{2,0,1:T(8,128)(2,1)S(1)}, u32[]{:S(2)}, u32[]{:S(2)}) async-start(bf16[64,32,128]{2,0,1:T(8,128)(2,1)} %bitcast.37), calls=%async_computation.1 | async-start | bytes 1048576 | tf_op jit(solution)/shard_map/all_to_all | solution.py:175
  44.3 42.9 %copy-start.21 = (bf16[64,32,128]{2,0,1:T(8,128)(2,1)}, bf16[64,32,128]{2,0,1:T(8,128)(2,1)S(1)}, u32[]{:S(2)}) copy-start(bf16[64,32,128]{2,0,1:T(8,128)(2,1)S(1)} %all-to-all-done.1) | copy-start | bytes 1572868
  45.3 19.4 %all-to-all-start.2 = ((bf16[64,32,128]{2,0,1:T(8,128)(2,1)}), bf16[64,32,128]{2,0,1:T(8,128)(2,1)S(1)}, u32[]{:S(2)}, u32[]{:S(2)}) async-start(bf16[64,32,128]{2,0,1:T(8,128)(2,1)} %bitcast.50), calls=%async_computation.2 | async-start | bytes 1048576 | tf_op jit(solution)/shard_map/all_to_all | solution.py:182
  65.7 19.4 %all-to-all-start.4 = ((bf16[64,32,128]{2,0,1:T(8,128)(2,1)}), bf16[64,32,128]{2,0,1:T(8,128)(2,1)S(1)}, u32[]{:S(2)}, u32[]{:S(2)}) async-start(bf16[64,32,128]{2,0,1:T(8,128)(2,1)} %bitcast.68), calls=%async_computation.4 | async-start | bytes 1048576 | tf_op jit(solution)/shard_map/all_to_all | solution.py:189
  87.2 66.4 %all-to-all-start = ((bf16[16,48,2048]{2,1,0:T(8,128)(2,1)}), bf16[16,48,2048]{2,1,0:T(8,128)(2,1)S(1)}, u32[]{:S(2)}, u32[]{:S(2)}) async-start(bf16[16,48,2048]{2,1,0:T(8,128)(2,1)} %broadcast_in_dim.186), calls=%async_computation | async-start | bytes 6291456 | tf_op jit(solution)/shard_map/all_to_all | solution.py:223
  156.2 50.6 %all-to-all-start.7 = ((bf16[64,32,352]{2,0,1:T(8,128)(2,1)}), bf16[64,32,352]{2,0,1:T(8,128)(2,1)}, u32[]{:S(2)}, u32[]{:S(2)}) async-start(bf16[64,32,352]{2,0,1:T(8,128)(2,1)} %bitcast.586), calls=%async_computation.7 | async-start | bytes 3145728 | tf_op jit(solution)/shard_map/all_to_all | solution.py:196
  186.2 3.9 collective-permute-start
  209.3 85.9 %all-to-all-start.8 = ((bf16[64,32,352]{2,0,1:T(8,128)(2,1)}), bf16[64,32,352]{2,0,1:T(8,128)(2,1)}, u32[]{:S(2)}, u32[]{:S(2)}) async-start(bf16[64,32,352]{2,0,1:T(8,128)(2,1)} %bitcast.585), calls=%async_computation.8 | async-start | bytes 3145728 | tf_op jit(solution)/shard_map/all_to_all | solution.py:203
  217.2 72.4 %copy-start.50 = (f32[128]{0:T(128)S(1)}, f32[128]{0:T(128)}, u32[]{:S(2)}) copy-start(f32[128]{0:T(128)} %param.26) | copy-start | bytes 1540
  295.2 69.1 %all-to-all-start.5 = ((bf16[16,48,2048]{2,1,0:T(8,128)(2,1)}), bf16[16,48,2048]{2,1,0:T(8,128)(2,1)}, u32[]{:S(2)}, u32[]{:S(2)}) async-start(bf16[16,48,2048]{2,1,0:T(8,128)(2,1)} %bitcast.582), calls=%async_computation.5 | async-start | bytes 6291456 | tf_op jit(solution)/shard_map/all_to_all | solution.py:262
  366.9 50.7 %all-to-all-start.9 = ((bf16[64,32,352]{2,0,1:T(8,128)(2,1)}), bf16[64,32,352]{2,0,1:T(8,128)(2,1)}, u32[]{:S(2)}, u32[]{:S(2)}) async-start(bf16[64,32,352]{2,0,1:T(8,128)(2,1)} %bitcast.589), calls=%async_computation.9 | async-start | bytes 3145728 | tf_op jit(solution)/shard_map/all_to_all | solution.py:210
  383.4 370.2 %copy-start.43 = (f32[48]{0:T(128)}, f32[48]{0:T(128)S(1)}, u32[]{:S(2)}) copy-start(f32[48]{0:T(128)S(1)} %fusion.120) | copy-start | bytes 580
  418.0 76.2 %copy-start.28 = (bf16[1,48,2048]{2,1,0:T(8,128)(2,1)S(1)}, bf16[1,48,2048]{2,1,0:T(8,128)(2,1)}, u32[]{:S(2)}) copy-start(bf16[1,48,2048]{2,1,0:T(8,128)(2,1)} %param.19) | copy-start | bytes 589828
  496.3 65.1 %all-to-all-start.11 = ((bf16[16,48,2048]{2,1,0:T(8,128)(2,1)}), bf16[16,48,2048]{2,1,0:T(8,128)(2,1)}, u32[]{:S(2)}, u32[]{:S(2)}) async-start(bf16[16,48,2048]{2,1,0:T(8,128)(2,1)} %broadcast_in_dim.210), calls=%async_computation.11 | async-start | bytes 6291456 | tf_op jit(solution)/shard_map/all_to_all | solution.py:276
  574.7 50.6 %all-to-all-start.21 = ((bf16[32,64,352]{2,1,0:T(8,128)(2,1)}), bf16[32,64,352]{2,1,0:T(8,128)(2,1)}, u32[]{:S(2)}, u32[]{:S(2)}) async-start(bf16[32,64,352]{2,1,0:T(8,128)(2,1)} %bitcast.590), calls=%async_computation.21 | async-start | bytes 3145728 | tf_op jit(solution)/shard_map/all_to_all | solution.py:360
  625.3 42.8 %all-to-all-start.19 = ((bf16[32,64,352]{2,1,0:T(8,128)(2,1)}), bf16[32,64,352]{2,1,0:T(8,128)(2,1)}, u32[]{:S(2)}, u32[]{:S(2)}) async-start(bf16[32,64,352]{2,1,0:T(8,128)(2,1)} %bitcast.588), calls=%async_computation.19 | async-start | bytes 3145728 | tf_op jit(solution)/shard_map/all_to_all | solution.py:354
  668.1 68.4 %all-to-all-start.12 = ((bf16[16,48,2048]{2,1,0:T(8,128)(2,1)}), bf16[16,48,2048]{2,1,0:T(8,128)(2,1)}, u32[]{:S(2)}, u32[]{:S(2)}) async-start(bf16[16,48,2048]{2,1,0:T(8,128)(2,1)} %bitcast.581), calls=%async_computation.12 | async-start | bytes 6291456 | tf_op jit(solution)/shard_map/all_to_all | solution.py:301
  736.5 50.6 %all-to-all-start.20 = ((bf16[32,64,352]{2,1,0:T(8,128)(2,1)}), bf16[32,64,352]{2,1,0:T(8,128)(2,1)}, u32[]{:S(2)}, u32[]{:S(2)}) async-start(bf16[32,64,352]{2,1,0:T(8,128)(2,1)} %bitcast.587), calls=%async_computation.20 | async-start | bytes 3145728 | tf_op jit(solution)/shard_map/all_to_all | solution.py:357
  753.6 36.5 %copy-start.48 = (f32[48]{0:T(128)}, f32[48]{0:T(128)S(1)}, u32[]{:S(2)}) copy-start(f32[48]{0:T(128)S(1)} %multiply_multiply_fusion.2) | copy-start | bytes 580
  790.1 68.4 %all-to-all-start.13 = ((bf16[16,48,2048]{2,1,0:T(8,128)(2,1)}), bf16[16,48,2048]{2,1,0:T(8,128)(2,1)}, u32[]{:S(2)}, u32[]{:S(2)}) async-start(bf16[16,48,2048]{2,1,0:T(8,128)(2,1)} %broadcast_in_dim.213), calls=%async_computation.13 | async-start | bytes 6291456 | tf_op jit(solution)/shard_map/all_to_all | solution.py:311
  858.6 75.0 %all-to-all-start.10 = ((bf16[16,48,2048]{2,1,0:T(8,128)(2,1)}), bf16[16,48,2048]{2,1,0:T(8,128)(2,1)}, u32[]{:S(2)}, u32[]{:S(2)}) async-start(bf16[16,48,2048]{2,1,0:T(8,128)(2,1)} %bitcast.597), calls=%async_computation.10 | async-start | bytes 6291456 | tf_op jit(solution)/shard_map/all_to_all | solution.py:282
  879.1 5.0 collective-permute-start.1
  933.5 154.7 %all-to-all-start.18 = ((bf16[32,64,128]{2,1,0:T(8,128)(2,1)}), bf16[32,64,128]{2,1,0:T(8,128)(2,1)}, u32[]{:S(2)}, u32[]{:S(2)}) async-start(bf16[32,64,128]{2,1,0:T(8,128)(2,1)} %bitcast.598), calls=%async_computation.18 | async-start | bytes 1048576 | tf_op jit(solution)/shard_map/all_to_all | solution.py:351
  1088.2 21.0 %all-to-all-start.17 = ((bf16[32,64,128]{2,1,0:T(8,128)(2,1)}), bf16[32,64,128]{2,1,0:T(8,128)(2,1)}, u32[]{:S(2)}, u32[]{:S(2)}) async-start(bf16[32,64,128]{2,1,0:T(8,128)(2,1)} %bitcast.599), calls=%async_computation.17 | async-start | bytes 1048576 | tf_op jit(solution)/shard_map/all_to_all | solution.py:348
  1109.2 20.1 %all-to-all-start.16 = ((bf16[32,64,128]{2,1,0:T(8,128)(2,1)}), bf16[32,64,128]{2,1,0:T(8,128)(2,1)}, u32[]{:S(2)}, u32[]{:S(2)}) async-start(bf16[32,64,128]{2,1,0:T(8,128)(2,1)} %bitcast.600), calls=%async_computation.16 | async-start | bytes 1048576 | tf_op jit(solution)/shard_map/all_to_all | solution.py:345
  1129.4 20.0 %all-to-all-start.15 = ((bf16[32,64,128]{2,1,0:T(8,128)(2,1)}), bf16[32,64,128]{2,1,0:T(8,128)(2,1)S(1)}, u32[]{:S(2)}, u32[]{:S(2)}) async-start(bf16[32,64,128]{2,1,0:T(8,128)(2,1)} %bitcast.114), calls=%async_computation.15 | async-start | bytes 1048576 | tf_op jit(solution)/shard_map/all_to_all | solution.py:342
  1150.2 98.1 %all-to-all-start.14 = ((bf16[16,48,2048]{2,1,0:T(8,128)(2,1)}), bf16[16,48,2048]{2,1,0:T(8,128)(2,1)S(1)}, u32[]{:S(2)}, u32[]{:S(2)}) async-start(bf16[16,48,2048]{2,1,0:T(8,128)(2,1)} %bitcast.583), calls=%async_computation.14 | async-start | bytes 6291456 | tf_op jit(solution)/shard_map/all_to_all | solution.py:330
  1245.0 47.6 %copy-start.1 = (bf16[64,2048]{1,0:T(8,128)(2,1)S(1)}, bf16[64,2048]{1,0:T(8,128)(2,1)}, u32[]{:S(2)}) copy-start(bf16[64,2048]{1,0:T(8,128)(2,1)} %param.22) | copy-start | bytes 786436
  (59 other events, 327.7 us)
where the time goes:
time: 1310 us; the launch traced here: 1290 us
  waiting for transfers between devices  547 us (42%)
  local copies, waits for them, and re-layouts  180 us (14%)
  starting transfers between devices  172 us (13%)
  matrix products  148 us (11%)
  blocking collectives  118 us (9%)
  other arithmetic  107 us (8%)
  loops' own time  16.2 us (1%)
    all_to_all x1, blocking collectives, body(): lax.all_to_all(fan_rows(second_low), 'hid', split_axis=0, concat_axis=0,...  76.2 us
    all_to_all x1, waiting for transfers between devices, body(): lax.all_to_all(times_t(head_low, o_block).astype(jnp.bfloat16), 'hid', sp...  56.8 us
    all_to_all x1, waiting for transfers between devices, body(): lax.all_to_all(fan_rows(mix_grad), 'hid', split_axis=0, concat_axis=0, ti...  56.3 us
    all_to_all x1, waiting for transfers between devices, body(): lax.all_to_all((times_t(gate_low, gate_block) + times_t(up_low, up_block)...  54.4 us
    all_to_all x1, waiting for transfers between devices, body(): lax.all_to_all(fan_rows(cotangent), 'hid', split_axis=0, concat_axis=0, t...  50.8 us
    all_to_all x1, waiting for transfers between devices, body(): lax.all_to_all(fan_rows(first_low), 'hid', split_axis=0, concat_axis=0, t...  50.7 us
    all_to_all x1, waiting for transfers between devices, body(): lax.all_to_all(times_t(hidden, down_block).astype(jnp.bfloat16), 'hid', s...  49.3 us
    convert_element_type x14, local copies, waits for them, and re-layouts, body(): q_back, f_back, i_back, o_back, gate_back, up_back, down_back = (lax.all_...  46.2 us
  transfers between devices with their start and end apart: 23, of which 18 were waited for; matrix products, arithmetic and copies ran while one was open for 31% of the time, Pallas kernels for 0%

commit v1 on v0

--- a/solution.py
+++ b/solution.py
@@ -1,6 +1,10 @@
+import functools
+
 import jax
 import jax.numpy as jnp
 from jax import lax
+from jax.experimental import pallas as pl
+from jax.experimental.pallas import tpu as pltpu
 from jax.sharding import PartitionSpec as P
 
 H = 16
@@ -27,15 +31,32 @@
     return (jax.nn.silu(q_part), key_gate, jnp.log1p(-key_gate))
 
 
+def doc_starts(lengths):
+    count = lengths.shape[0]
+    earlier = lax.broadcasted_iota(jnp.int32, (count, count), 0) > lax.broadcasted_iota(
+        jnp.int32, (count, count), 1
+    )
+    return jnp.sum(jnp.where(earlier, lengths[None, :], 0), axis=1)
+
+
+def running_sum(rows):
+    extent = rows.shape[-2]
+    lower = (
+        lax.broadcasted_iota(jnp.int32, (extent, extent), 0)
+        >= lax.broadcasted_iota(jnp.int32, (extent, extent), 1)
+    ).astype(jnp.float32)
+    return jnp.einsum("ts,...sk->...tk", lower, rows, precision=HIGH_PRECISION)
+
+
 def doc_ids(lengths, positions):
-    starts = jnp.cumsum(lengths) - lengths
+    starts = doc_starts(lengths)
     covered = (starts[None, :] <= positions[:, None]).astype(jnp.int32)
     return jnp.sum(covered, axis=1) - 1
 
 
 def span_step(memory_state, pieces):
     queries, key_gate, value_rows, log_decay, documents, before = pieces
-    cumulative = jnp.cumsum(log_decay, axis=1)
+    cumulative = running_sum(log_decay)
     query_decayed = queries * jnp.exp(cumulative)
     k_grown = key_gate * jnp.exp(-cumulative)
     extent = documents.shape[0]
@@ -138,7 +159,7 @@
     )
 
 
-def body(
+def wide_body(
     inputs,
     cotangent,
     lengths,
@@ -226,7 +247,7 @@
     i_lin = jnp.dot(first_rows, i_block, preferred_element_type=jnp.float32)
     gap_part = lax.dynamic_slice_in_dim(gap_log, head_id * head_width, head_width)
     queries, key_gate, log_decay = gates(q_lin, f_lin, gap_part)
-    cumulative = jnp.cumsum(log_decay, axis=0)
+    cumulative = running_sum(log_decay)
     last_cum = cumulative[-1]
     tail_key_rows = (
         jnp.exp(last_cum[None, :] - cumulative)
@@ -384,6 +405,772 @@
     )
 
 
+F32 = jnp.float32
+BF = jnp.bfloat16
+MESH = pl.DeviceIdType.MESH
+DMA = pltpu.SemaphoreType.DMA
+VMEM = pltpu.VMEM
+SUBS = 3
+LAG = 2
+VSPEC = pl.BlockSpec(memory_space=pltpu.VMEM)
+ASPEC = pl.BlockSpec(memory_space=pl.ANY)
+SSPEC = pl.BlockSpec(memory_space=pltpu.SMEM)
+
+
+def place():
+    h = lax.axis_index("hid")
+    return h, h // 4, lax.rem(h // 2, 2), lax.rem(h, 2)
+
+
+def partners():
+    h, z, y, x = place()
+    column = [lax.rem(z + k, 4) * 4 + lax.rem(h, 4) for k in (1, 2, 3)]
+    return column, h + 2 - 4 * y, h + 1 - 2 * x
+
+
+def greet(chips, core=False):
+    gate = pltpu.get_barrier_semaphore()
+    for chip in chips:
+        pl.semaphore_signal(gate, inc=1, device_id={"hid": chip}, device_id_type=MESH)
+    if core:
+        other = 1 - lax.axis_index("seq")
+        pl.semaphore_signal(gate, inc=1, device_id={"seq": other}, device_id_type=MESH)
+    pl.semaphore_wait(gate, len(chips) + int(core))
+
+
+def to_chip(src, dst, send, recv, chip):
+    return pltpu.make_async_remote_copy(
+        src_ref=src,
+        dst_ref=dst,
+        send_sem=send,
+        recv_sem=recv,
+        device_id={"hid": chip},
+        device_id_type=MESH,
+    )
+
+
+def to_core(src, dst, send, recv):
+    return pltpu.make_async_remote_copy(
+        src_ref=src,
+        dst_ref=dst,
+        send_sem=send,
+        recv_sem=recv,
+        device_id={"seq": 1 - lax.axis_index("seq")},
+        device_id_type=MESH,
+    )
+
+
+def comm_params(collective_id):
+    return pltpu.CompilerParams(
+        collective_id=collective_id, has_side_effects=True, vmem_limit_bytes=48 << 20
+    )
+
+
+def cut_list():
+    return [(i, j) for i in range(SUBS) for j in range(2)]
+
+
+def gather_kernel(x_ref, o_ref, s1, r1, s2, r2, s3, r3, ls):
+    h, z, y, x = place()
+    column, py, px = partners()
+    rows, half = x_ref.shape[0] // SUBS, x_ref.shape[1] // 2
+    greet(column + [py, px])
+    cuts = cut_list()
+
+    def cut(i, j):
+        return pl.ds(i * rows, rows), pl.ds(j * half, half)
+
+    own = pltpu.make_async_copy(x_ref, o_ref.at[z, y, x], ls)
+    own.start()
+    c1, c2, c3 = {}, {}, {}
+    for c, (i, j) in enumerate(cuts):
+        a, b = cut(i, j)
+        for k in range(3):
+            c1[c, k] = to_chip(
+                x_ref.at[a, b], o_ref.at[z, y, x, a, b], s1.at[c, k], r1.at[c, k], column[k]
+            )
+            c1[c, k].start()
+    own.wait()
+    n = len(cuts)
+    for t in range(n + LAG):
+        if t < n:
+            i, j = cuts[t]
+            a, b = cut(i, j)
+            for k in range(3):
+                c1[t, k].wait_recv()
+            ref = o_ref.at[:, y, x, a, b]
+            c2[t] = to_chip(ref, ref, s2.at[t], r2.at[t], py if j else px)
+            c2[t].start()
+        if t >= LAG:
+            c = t - LAG
+            i, j = cuts[c]
+            a, b = cut(i, j)
+            c2[c].wait_recv()
+            ref = o_ref.at[:, :, x, a, b] if j else o_ref.at[:, y, :, a, b]
+            c3[c] = to_chip(ref, ref, s3.at[c], r3.at[c], px if j else py)
+            c3[c].start()
+    for c in range(n):
+        c3[c].wait_recv()
+    for c in range(n):
+        for k in range(3):
+            c1[c, k].wait_send()
+        c2[c].wait_send()
+        c3[c].wait_send()
+
+
+def gather_rows(local, collective_id):
+    n = 2 * SUBS
+    out = pl.pallas_call(
+        gather_kernel,
+        out_shape=jax.ShapeDtypeStruct((4, 2, 2) + local.shape, local.dtype),
+        in_specs=[VSPEC],
+        out_specs=VSPEC,
+        scratch_shapes=[DMA((n, 3)), DMA((n, 3)), DMA((n,)), DMA((n,)), DMA((n,)), DMA((n,)), DMA],
+        compiler_params=comm_params(collective_id),
+    )(local)
+    return out.reshape(H * local.shape[0], local.shape[1])
+
+
+def scatter_kernel(p_ref, o_ref, b1, t1, b2, t2, b3, s1, r1, s2, r2, s3, r3):
+    h, z, y, x = place()
+    column, py, px = partners()
+    rows, half = o_ref.shape[0] // SUBS, o_ref.shape[1] // 2
+    greet(column + [py, px])
+    cuts = cut_list()
+
+    def cut(i, j):
+        return pl.ds(i * rows, rows), pl.ds(j * half, half)
+
+    c1, c2, c3 = {}, {}, {}
+    for c, (i, j) in enumerate(cuts):
+        a, b = cut(i, j)
+        src = p_ref.at[:, :, 1 - x, a, b] if j else p_ref.at[:, 1 - y, :, a, b]
+        c1[c] = to_chip(src, b1.at[c], s1.at[c], r1.at[c], px if j else py)
+        c1[c].start()
+
+    def second(c):
+        i, j = cuts[c]
+        a, b = cut(i, j)
+        c1[c].wait_recv()
+        mine = p_ref[:, :, x, a, b] if j else p_ref[:, y, :, a, b]
+        t1[c] = mine.astype(F32) + b1[c].astype(F32)
+        q = y if j else x
+        b1[c, :, 0] = t1[c, :, 1 - q].astype(BF)
+        c2[c] = to_chip(b1.at[c, :, 0], b2.at[c], s2.at[c], r2.at[c], py if j else px)
+        c2[c].start()
+
+    def third(c):
+        i, j = cuts[c]
+        c2[c].wait_recv()
+        q = y if j else x
+        t2[c] = t1[c, :, q] + b2[c].astype(F32)
+        b2[c] = t2[c].astype(BF)
+        for k in range(3):
+            c3[c, k] = to_chip(
+                b2.at[c, lax.rem(z + k + 1, 4)],
+                b3.at[c, k],
+                s3.at[c, k],
+                r3.at[c, k],
+                column[k],
+            )
+            c3[c, k].start()
+
+    def last(c):
+        i, j = cuts[c]
+        a, b = cut(i, j)
+        for k in range(3):
+            c3[c, k].wait_recv()
+        o_ref[a, b] = t2[c, z] + b3[c, 0].astype(F32) + b3[c, 1].astype(F32) + b3[c, 2].astype(F32)
+
+    n = len(cuts)
+    for t in range(n + 2 * LAG):
+        if t < n:
+            second(t)
+        if 0 <= t - LAG < n:
+            third(t - LAG)
+        if 0 <= t - 2 * LAG < n:
+            last(t - 2 * LAG)
+    for c in range(n):
+        c1[c].wait_send()
+        c2[c].wait_send()
+        for k in range(3):
+            c3[c, k].wait_send()
+
+
+def scatter_rows(part, collective_id):
+    n, rows, cols = 2 * SUBS, part.shape[0] // H, part.shape[1]
+    r, w = rows // SUBS, cols // 2
+    return pl.pallas_call(
+        scatter_kernel,
+        out_shape=jax.ShapeDtypeStruct((rows, cols), F32),
+        in_specs=[VSPEC],
+        out_specs=VSPEC,
+        scratch_shapes=[
+            VMEM((n, 4, 2, r, w), BF),
+            VMEM((n, 4, 2, r, w), F32),
+            VMEM((n, 4, r, w), BF),
+            VMEM((n, 4, r, w), F32),
+            VMEM((n, 3, r, w), BF),
+            DMA((n,)),
+            DMA((n,)),
+            DMA((n,)),
+            DMA((n,)),
+            DMA((n, 3)),
+            DMA((n, 3)),
+        ],
+        compiler_params=comm_params(collective_id),
+    )(part.reshape(4, 2, 2, rows, cols))
+
+
+def unit_span(tiles, h):
+    first = (tiles * h) // H
+    return first, (tiles * (h + 1)) // H - first
+
+
+def lanes(tile, count):
+    return pl.ds(pl.multiple_of(tile * 128, 128), count * 128)
+
+
+def sized(tiles, h, act):
+    least = tiles // H
+    if tiles % H == 0:
+        act(least)
+        return
+    _, count = unit_span(tiles, h)
+    for number in (least, least + 1):
+        pl.when(count == number)(functools.partial(act, number))
+
+
+def weights_kernel(tiles, q, f, i, o, g, u, d, wqfi, wo, wg, wu, wd, ss, rs, ls, xs, xr):
+    h, b = lax.axis_index("hid"), lax.axis_index("seq")
+    greet([lax.rem(h + k, H) for k in range(1, H)], core=True)
+    depth = q.shape[0]
+    mine = pl.ds(pl.multiple_of((b * H + h) * depth, depth), depth)
+    heads = [(q, wqfi, 0), (f, wqfi, 1), (i, wqfi, 2), (o, wo, 0)]
+    units = [(g, wg), (u, wu), (d, wd)]
+
+    def head_copy(n, k, chip):
+        src, dst, at = heads[n]
+        return to_chip(
+            src.at[:, lanes(chip, 1)], dst.at[mine, lanes(at, 1)], ss.at[n, k], rs.at[n, k], chip
+        )
+
+    def unit_copy(n, k, chip, count):
+        src, dst = units[n]
+        first, _ = unit_span(tiles, chip)
+        return to_chip(
+            src.at[:, lanes(first, count)],
+            dst.at[mine, lanes(0, count)],
+            ss.at[4 + n, k],
+            rs.at[4 + n, k],
+            chip,
+        )
+
+    for n in range(4):
+        for k in range(1, H):
+            head_copy(n, k, lax.rem(h + k, H)).start()
+    for n in range(3):
+        for k in range(1, H):
+            chip = lax.rem(h + k, H)
+            sized(tiles, chip, lambda count: unit_copy(n, k, chip, count).start())
+    own = [
+        pltpu.make_async_copy(src.at[:, lanes(h, 1)], dst.at[mine, lanes(at, 1)], ls.at[n])
+        for n, (src, dst, at) in enumerate(heads)
+    ]
+    for copy in own:
+        copy.start()
+
+    def own_units(act):
+        def run(count):
+            for n, (src, dst) in enumerate(units):
+                first, _ = unit_span(tiles, h)
+                act(
+                    pltpu.make_async_copy(
+                        src.at[:, lanes(first, count)], dst.at[mine, lanes(0, count)], ls.at[4 + n]
+                    )
+                )
+
+        sized(tiles, h, run)
+
+    own_units(lambda copy: copy.start())
+    wide = wg.shape[1] // 128
+    if tiles % H:
+
+        @pl.when(unit_span(tiles, h)[1] < wide)
+        def _():
+            for _, dst in units:
+                dst[:, (wide - 1) * 128 :] = jnp.zeros((dst.shape[0], 128), BF)
+
+    for copy in own:
+        copy.wait()
+    own_units(lambda copy: copy.wait())
+    half = wqfi.shape[0] // 2
+    ours = pl.ds(pl.multiple_of(b * half, half), half)
+    swaps = []
+
+    def swap(n, ref, cols=None):
+        view = ref.at[ours] if cols is None else ref.at[ours, cols]
+        copy = to_core(view, view, xs.at[n], xr.at[n])
+        copy.start()
+        swaps.append(copy)
+
+    for n in range(3):
+        for k in range(1, H):
+            head_copy(n, k, h).wait_recv()
+    swap(0, wqfi)
+    for k in range(1, H):
+        head_copy(3, k, h).wait_recv()
+    swap(1, wo)
+    for n in range(3):
+        for k in range(1, H):
+            sized(tiles, h, lambda count: unit_copy(n, k, h, count).wait_recv())
+        least = tiles // H
+        if tiles % H == 0:
+            swap(2 + n, units[n][1])
+        else:
+            ref = units[n][1].at[ours, pl.ds(0, least * 128)]
+            copy = to_core(ref, ref, xs.at[2 + n], xr.at[2 + n])
+            copy.start()
+            swaps.append(copy)
+
+            @pl.when(unit_span(tiles, h)[1] > least)
+            def _():
+                more = units[n][1].at[ours, pl.ds(least * 128, 128)]
+                to_core(more, more, xs.at[5 + n], xr.at[5 + n]).start()
+
+    for copy in swaps:
+        copy.wait()
+    if tiles % H:
+
+        @pl.when(unit_span(tiles, h)[1] > least)
+        def _():
+            for n in range(3):
+                more = units[n][1].at[ours, pl.ds(least * 128, 128)]
+                to_core(more, more, xs.at[5 + n], xr.at[5 + n]).wait()
+
+    for n in range(4):
+        for k in range(1, H):
+            head_copy(n, k, lax.rem(h + k, H)).wait_send()
+    for n in range(3):
+        for k in range(1, H):
+            chip = lax.rem(h + k, H)
+            sized(tiles, chip, lambda count: unit_copy(n, k, chip, count).wait_send())
+
+
+def fetch_weights(weights, collective_id):
+    depth, model = weights[0].shape
+    rows, tiles = 2 * H * depth, weights[4].shape[1] // 128
+    wide = -(-tiles // H) * 128
+    shape = lambda cols: jax.ShapeDtypeStruct((rows, cols), BF)
+    return pl.pallas_call(
+        functools.partial(weights_kernel, tiles),
+        out_shape=[shape(384), shape(128), shape(wide), shape(wide), shape(wide)],
+        in_specs=[ASPEC] * 7,
+        out_specs=[VSPEC] * 5,
+        scratch_shapes=[DMA((7, H)), DMA((7, H)), DMA((7,)), DMA((8,)), DMA((8,))],
+        compiler_params=comm_params(collective_id),
+    )(*weights)
+
+
+def grads_kernel(tiles, pqfi, po, pg, pu, pd, q, f, i, o, g, u, d, rq, ro, rg, ru, rd, *sems):
+    ss, rs, ls, xs, xr = sems
+    h, b = lax.axis_index("hid"), lax.axis_index("seq")
+    greet([lax.rem(h + k, H) for k in range(1, H)], core=True)
+    parts, sums = [pqfi, po, pg, pu, pd], [rq, ro, rg, ru, rd]
+    half = pqfi.shape[0] // 2
+    ours = pl.ds(pl.multiple_of(b * half, half), half)
+    theirs = pl.ds(pl.multiple_of((1 - b) * half, half), half)
+    order = [4, 2, 3, 1, 0]
+    swaps = {n: to_core(parts[n].at[theirs], sums[n], xs.at[n], xr.at[n]) for n in order}
+    for n in order:
+        swaps[n].start()
+    depth = half // H
+    heads = [(rq, 0, q), (rq, 1, f), (rq, 2, i), (ro, 0, o)]
+    units = [(rg, g), (ru, u), (rd, d)]
+
+    def rows_of(chip):
+        return pl.ds(pl.multiple_of(chip * depth, depth), depth)
+
+    def head_copy(n, k, chip, source):
+        src, at, dst = heads[n]
+        return to_chip(
+            src.at[rows_of(chip), lanes(at, 1)],
+            dst.at[:, lanes(source, 1)],
+            ss.at[n, k],
+            rs.at[n, k],
+            chip,
+        )
+
+    def unit_copy(n, k, chip, source, count):
+        src, dst = units[n]
+        first, _ = unit_span(tiles, source)
+        return to_chip(
+            src.at[rows_of(chip), lanes(0, count)],
+            dst.at[:, lanes(first, count)],
+            ss.at[4 + n, k],
+            rs.at[4 + n, k],
+            chip,
+        )
+
+    def add(n):
+        swaps[n].wait()
+        step = 64
+
+        @pl.loop(0, half // step)
+        def _(t):
+            at = pl.ds(pl.multiple_of(t * step, step), step)
+            own = pl.ds(pl.multiple_of(b * half + t * step, step), step)
+            sums[n][at] = (sums[n][at].astype(F32) + parts[n][own].astype(F32)).astype(BF)
+
+    def own_heads(ns, act):
+        for n in ns:
+            src, at, dst = heads[n]
+            act(
+                pltpu.make_async_copy(
+                    src.at[rows_of(h), lanes(at, 1)], dst.at[:, lanes(h, 1)], ls.at[n]
+                )
+            )
+
+    def own_unit(n, act):
+        src, dst = units[n]
+
+        def run(count):
+            first, _ = unit_span(tiles, h)
+            act(
+                pltpu.make_async_copy(
+                    src.at[rows_of(h), lanes(0, count)], dst.at[:, lanes(first, count)], ls.at[4 + n]
+                )
+            )
+
+        sized(tiles, h, run)
+
+    for n in order:
+        add(n)
+        if n >= 2:
+            for k in range(1, H):
+                chip = lax.rem(h + k, H)
+                sized(tiles, h, lambda count: unit_copy(n - 2, k, chip, h, count).start())
+            own_unit(n - 2, lambda copy: copy.start())
+        else:
+            for m in (3,) if n else (0, 1, 2):
+                for k in range(1, H):
+                    head_copy(m, k, lax.rem(h + k, H), h).start()
+            own_heads((3,) if n else (0, 1, 2), lambda copy: copy.start())
+    own_heads(range(4), lambda copy: copy.wait())
+    for n in range(3):
+        own_unit(n, lambda copy: copy.wait())
+    for k in range(1, H):
+        chip, source = lax.rem(h + k, H), lax.rem(h + H - k, H)
+        for n in range(4):
+            head_copy(n, k, chip, source).wait_recv()
+            head_copy(n, k, chip, h).wait_send()
+        for n in range(3):
+            sized(
+                tiles, source, lambda count: unit_copy(n, k, chip, source, count).wait_recv()
+            )
+            sized(tiles, h, lambda count: unit_copy(n, k, chip, h, count).wait_send())
+
+
+def return_grads(parts, model, units, collective_id):
+    rows, tiles = parts[0].shape[0], units // 128
+    depth = rows // (2 * H)
+    shape = lambda cols: jax.ShapeDtypeStruct((depth, cols), BF)
+    return pl.pallas_call(
+        functools.partial(grads_kernel, tiles),
+        out_shape=[shape(model)] * 4 + [shape(units)] * 3,
+        in_specs=[VSPEC] * 5,
+        out_specs=[VSPEC] * 7,
+        scratch_shapes=[VMEM((rows // 2, p.shape[1]), BF) for p in parts]
+        + [DMA((7, H)), DMA((7, H)), DMA((7,)), DMA((5,)), DMA((5,))],
+        compiler_params=comm_params(collective_id),
+    )(*parts)
+
+
+def mm(left, right, at_left, at_right):
+    return lax.dot_general(
+        left.astype(BF),
+        right.astype(BF),
+        (((at_left,), (at_right,)), ((), ())),
+        preferred_element_type=F32,
+    )
+
+
+def tri_sum(rows, reverse=False):
+    r = lax.broadcasted_iota(jnp.int32, (SPAN, SPAN), 0)
+    c = lax.broadcasted_iota(jnp.int32, (SPAN, SPAN), 1)
+    picked = jnp.where((r <= c) if reverse else (r >= c), 1.0, 0.0).astype(BF)
+    high = rows.astype(BF)
+    rest = rows - high.astype(F32)
+    middle = rest.astype(BF)
+    low = rest - middle.astype(F32)
+    return mm(picked, high, 1, 0) + mm(picked, middle, 1, 0) + mm(picked, low, 1, 0)
+
+
+def span_gates(lin_ref, gap_ref, at):
+    q_lin, f_lin, values = lin_ref[at, 0:128], lin_ref[at, 128:256], lin_ref[at, 256:384]
+    s = jax.nn.sigmoid(q_lin)
+    key = jnp.exp(gap_ref[...]) * jax.nn.sigmoid(-f_lin)
+    return q_lin, f_lin, values, s, key
+
+
+def span_masks(dcol_ref, drow_ref, marks_ref, c, at):
+    r = lax.broadcasted_iota(jnp.int32, (SPAN, SPAN), 0)
+    k = lax.broadcasted_iota(jnp.int32, (SPAN, SPAN), 1)
+    dcol, drow = dcol_ref[at], drow_ref[c : c + 1]
+    before, end = marks_ref[0, c], marks_ref[1, c]
+    same = jnp.where(jnp.logical_and(dcol == drow, r >= k), 1.0, 0.0)
+    carried = jnp.where(dcol == before, 1.0, 0.0)
+    keep = jnp.where(dcol == end, 1.0, 0.0)
+    whole = jnp.where(end == before, 1.0, 0.0)
+    return same, carried, keep, whole
+
+
+def spans(extent):
+    return [(c, pl.ds(c * SPAN, SPAN)) for c in range(extent // SPAN)]
+
+
+def mix_kernel(
+    lin_ref, gap_ref, gain_ref, dcol_ref, drow_ref, marks_ref,
+    mixed_ref, states_ref, head_ref, cum_ref, out_ref, in_ref, send, recv,
+):
+    greet([], core=True)
+    extent = lin_ref.shape[0]
+    steps = spans(extent)
+    state = jnp.zeros((SPAN, SPAN), F32)
+    for c, at in steps:
+        q_lin, f_lin, values, s, key = span_gates(lin_ref, gap_ref, at)
+        same, carried, keep, whole = span_masks(dcol_ref, drow_ref, marks_ref, c, at)
+        cum = tri_sum(jnp.log1p(-key))
+        cum_ref[at] = cum
+        end = cum[SPAN - 1 : SPAN]
+        fresh = mm(values, jnp.exp(end - cum) * key * keep, 0, 0)
+        states_ref[c] = fresh
+        state = state * (jnp.exp(end) * whole) + fresh
+    out_ref[...] = state
+    copy = to_core(out_ref, in_ref, send, recv)
+    copy.start()
+    copy.wait()
+    state = in_ref[...] * lax.axis_index("seq").astype(F32)
+    for c, at in steps:
+        q_lin, f_lin, values, s, key = span_gates(lin_ref, gap_ref, at)
+        same, carried, keep, whole = span_masks(dcol_ref, drow_ref, marks_ref, c, at)
+        cum = cum_ref[at]
+        end = cum[SPAN - 1 : SPAN]
+        fresh = states_ref[c]
+        states_ref[c] = state
+        decayed = q_lin * s * jnp.exp(cum)
+        scores = mm(decayed, key * jnp.exp(-cum), 1, 1) * same
+        mixed = mm(scores, values, 1, 0) + carried * mm(decayed, state, 1, 1)
+        mixed_ref[at] = mixed
+        factor = lax.rsqrt(jnp.mean(mixed * mixed, axis=-1, keepdims=True) + EPS)
+        head_ref[at] = (mixed * factor * gain_ref[...]).astype(BF)
+        state = state * (jnp.exp(end) * whole) + fresh
+
+
+def mix_forward(lin, gap_row, gain_row, dcol, drow, marks, collective_id):
+    extent = lin.shape[0]
+    tile = jax.ShapeDtypeStruct((extent, SPAN), F32)
+    return pl.pallas_call(
+        mix_kernel,
+        out_shape=[
+            tile,
+            jax.ShapeDtypeStruct((extent // SPAN, SPAN, SPAN), F32),
+            jax.ShapeDtypeStruct((extent, SPAN), BF),
+            tile,
+        ],
+        in_specs=[VSPEC] * 5 + [SSPEC],
+        out_specs=[VSPEC] * 4,
+        scratch_shapes=[VMEM((SPAN, SPAN), F32), VMEM((SPAN, SPAN), F32), DMA, DMA],
+        compiler_params=comm_params(collective_id),
+    )(lin, gap_row, gain_row, dcol, drow, marks)
+
+
+def unmix_kernel(
+    lin_ref, gap_ref, gain_ref, dcol_ref, drow_ref, marks_ref, mixed_ref, states_ref, cum_ref, dhead_ref,
+    dlin_ref, gapg_ref, groupg_ref, do_ref, back_ref, out_ref, in_ref, send, recv,
+):
+    greet([], core=True)
+    extent = lin_ref.shape[0]
+    steps = spans(extent)
+    group = jnp.zeros((1, SPAN), F32)
+    adjoint = jnp.zeros((SPAN, SPAN), F32)
+    for c, at in reversed(steps):
+        mixed, dy = mixed_ref[at], dhead_ref[at]
+        factor = lax.rsqrt(jnp.mean(mixed * mixed, axis=-1, keepdims=True) + EPS)
+        normal = mixed * factor
+        group = group + jnp.sum(dy * normal, axis=0, keepdims=True)
+        scaled = dy * gain_ref[...]
+        d_mixed = factor * (scaled - normal * jnp.mean(scaled * normal, axis=-1, keepdims=True))
+        do_ref[at] = d_mixed
+        q_lin, f_lin, values, s, key = span_gates(lin_ref, gap_ref, at)
+        same, carried, keep, whole = span_masks(dcol_ref, drow_ref, marks_ref, c, at)
+        cum = cum_ref[at]
+        back = mm(d_mixed, carried * (q_lin * s * jnp.exp(cum)), 0, 0)
+        back_ref[c] = back
+        adjoint = adjoint * (jnp.exp(cum[SPAN - 1 : SPAN]) * whole) + back
+    groupg_ref[...] = group
+    out_ref[...] = adjoint
+    copy = to_core(out_ref, in_ref, send, recv)
+    copy.start()
+    copy.wait()
+    adjoint = in_ref[...] * (1 - lax.axis_index("seq")).astype(F32)
+    gap = jnp.zeros((1, SPAN), F32)
+    for c, at in reversed(steps):
+        q_lin, f_lin, values, s, key = span_gates(lin_ref, gap_ref, at)
+        same, carried, keep, whole = span_masks(dcol_ref, drow_ref, marks_ref, c, at)
+        cum, d_mixed, state = cum_ref[at], do_ref[at], states_ref[c]
+        grow, shrink = jnp.exp(-cum), jnp.exp(cum)
+        end = cum[SPAN - 1 : SPAN]
+        decayed, grown = q_lin * s * shrink, key * grow
+        rest = jnp.exp(end - cum) * keep
+        tail, through = rest * key, jnp.exp(end) * whole
+        scores = mm(decayed, grown, 1, 1) * same
+        d_scores = mm(d_mixed, values, 1, 1) * same
+        d_values = mm(scores, d_mixed, 0, 0) + mm(tail, adjoint, 1, 1)
+        d_decayed = mm(d_scores, grown, 1, 0) + carried * mm(d_mixed, state, 1, 0)
+        d_grown = mm(d_scores, decayed, 0, 0)
+        d_tail = mm(values, adjoint, 1, 0)
+        held = tail * d_tail
+        d_cum = decayed * d_decayed - grown * d_grown - held
+        d_end = jnp.sum(held, axis=0, keepdims=True) + through * jnp.sum(
+            state * adjoint, axis=0, keepdims=True
+        )
+        d_log = tri_sum(d_cum, reverse=True) + d_end
+        d_key = d_grown * grow + d_tail * rest - d_log / (1.0 - key)
+        scaled = d_key * key
+        gap = gap + jnp.sum(scaled, axis=0, keepdims=True)
+        dlin_ref[at, 0:128] = (d_decayed * shrink * s * (1.0 + q_lin * (1.0 - s))).astype(BF)
+        dlin_ref[at, 128:256] = (-scaled * jax.nn.sigmoid(f_lin)).astype(BF)
+        dlin_ref[at, 256:384] = d_values.astype(BF)
+        adjoint = adjoint * through + back_ref[c]
+    gapg_ref[...] = gap
+
+
+def mix_backward(lin, gap_row, gain_row, dcol, drow, marks, mixed, states, cum, d_head, collective_id):
+    extent = lin.shape[0]
+    row = jax.ShapeDtypeStruct((1, SPAN), F32)
+    return pl.pallas_call(
+        unmix_kernel,
+        out_shape=[jax.ShapeDtypeStruct(lin.shape, BF), row, row],
+        in_specs=[VSPEC] * 5 + [SSPEC] + [VSPEC] * 4,
+        out_specs=[VSPEC] * 3,
+        scratch_shapes=[
+            VMEM((extent, SPAN), F32),
+            VMEM((extent // SPAN, SPAN, SPAN), F32),
+            VMEM((SPAN, SPAN), F32),
+            VMEM((SPAN, SPAN), F32),
+            DMA,
+            DMA,
+        ],
+        compiler_params=comm_params(collective_id),
+    )(lin, gap_row, gain_row, dcol, drow, marks, mixed, states, cum, d_head)
+
+
+def dot_low(left, right):
+    return jnp.dot(left, right, preferred_element_type=F32).astype(BF)
+
+
+def fast_body(
+    inputs,
+    cotangent,
+    lengths,
+    first_gain,
+    q_weight,
+    f_weight,
+    i_weight,
+    o_weight,
+    group_gain,
+    gap_log,
+    second_gain,
+    gate_weight,
+    up_weight,
+    down_weight,
+):
+    rows, model = inputs.shape[1:]
+    units = gate_weight.shape[1]
+    head_id, block_id = lax.axis_index("hid"), lax.axis_index("seq")
+    block_len = H * rows
+    entries = inputs[0].astype(F32)
+    cot_low = cotangent[0]
+    positions = block_id * block_len + lax.iota(jnp.int32, block_len)
+    documents = doc_ids(lengths, positions)
+    before = doc_ids(lengths, jnp.reshape(block_id * block_len - 1, (1,)))
+    drow = documents.reshape(block_len // SPAN, SPAN)
+    ends = drow[:, -1]
+    marks = jnp.stack([jnp.concatenate([before, ends[:-1]]), ends])
+    gap_row = lax.dynamic_slice_in_dim(gap_log, head_id * SPAN, SPAN)[None]
+    gain_row = group_gain[None]
+    aids = (gap_row, gain_row, documents[:, None], drow, marks)
+
+    first_norm, first_back = jax.vjp(normed, entries, first_gain)
+    qfi_block, o_block, gate_block, up_block, down_block = fetch_weights(
+        (q_weight, f_weight, i_weight, o_weight, gate_weight, up_weight, down_weight), 1
+    )
+    first_rows = gather_rows(first_norm.astype(BF), 2)
+    cot_rows = gather_rows(cot_low, 2)
+    lin = jnp.dot(first_rows, qfi_block, preferred_element_type=F32)
+    mixed, states, head_low, cum = mix_forward(lin, *aids, 3)
+    mix_out = scatter_rows(times_t(head_low, o_block).astype(BF), 4)
+    middle = entries + mix_out
+    second_norm, second_back = jax.vjp(normed, middle, second_gain)
+    second_rows = gather_rows(second_norm.astype(BF), 2)
+    gate_lin = jnp.dot(second_rows, gate_block, preferred_element_type=F32)
+    up_lin = jnp.dot(second_rows, up_block, preferred_element_type=F32)
+    gate_sig = jax.nn.sigmoid(gate_lin)
+    hidden = (gate_lin * gate_sig * up_lin).astype(BF)
+    hidden_grad = jnp.dot(cot_rows, down_block, preferred_element_type=F32)
+    gate_low = (hidden_grad * up_lin * gate_sig * (1.0 + gate_lin * (1.0 - gate_sig))).astype(BF)
+    up_low = (hidden_grad * gate_lin * gate_sig).astype(BF)
+    second_sum = scatter_rows(
+        (times_t(gate_low, gate_block) + times_t(up_low, up_block)).astype(BF), 4
+    )
+    middle_part, second_part = second_back(second_sum)
+    middle_grad = cot_low.astype(F32) + middle_part
+    mix_rows = gather_rows(middle_grad.astype(BF), 2)
+    d_head = jnp.dot(mix_rows, o_block, preferred_element_type=F32)
+    d_lin, gap_part, group_part = mix_backward(lin, *aids, mixed, states, cum, d_head, 5)
+    first_sum = scatter_rows(times_t(d_lin, qfi_block).astype(BF), 4)
+    entry_part, first_part = first_back(first_sum)
+    input_grad = middle_grad + entry_part
+    glu_out = scatter_rows(times_t(hidden, down_block).astype(BF), 4)
+    output = (middle + glu_out).astype(BF)
+    grads = return_grads(
+        (
+            outer_sum(first_rows, d_lin).astype(BF),
+            outer_sum(mix_rows, head_low).astype(BF),
+            outer_sum(second_rows, gate_low).astype(BF),
+            outer_sum(second_rows, up_low).astype(BF),
+            outer_sum(cot_rows, hidden).astype(BF),
+        ),
+        model,
+        units,
+        6,
+    )
+    q_grad, f_grad, i_grad, o_grad, gate_grad, up_grad, down_grad = (
+        grad.astype(F32) for grad in grads
+    )
+    head_pick = (lax.iota(jnp.int32, H) == head_id).astype(F32)
+    gap_full = (head_pick[:, None] * gap_part).reshape(model)
+    first_grad, second_grad, group_grad, gap_grad = lax.psum(
+        (first_part, second_part, group_part[0], gap_full), ("seq", "hid")
+    )
+    return (
+        output[None],
+        input_grad[None],
+        first_grad,
+        q_grad,
+        f_grad,
+        i_grad,
+        o_grad,
+        group_grad,
+        gap_grad,
+        second_grad,
+        gate_grad,
+        up_grad,
+        down_grad,
+    )
+
+
 def solution(mesh):
     placed = (
         P("seq", "hid", None),
@@ -401,6 +1188,7 @@
         P(("seq", "hid"), None),
         P(("seq", "hid"), None),
     )
+    body = fast_body if mesh.shape["hid"] == H else wide_body
     return jax.shard_map(
         body,
         mesh=mesh,

time: 1310 us -> 576 us (0.44)
  waiting for transfers between devices: 547 us -> 0 us
  Pallas kernels: 0 us -> 480 us
  local copies, waits for them, and re-layouts: 180 us -> 1.4 us
  starting transfers between devices: 172 us -> 0 us
  matrix products: 148 us -> 30.4 us
  other arithmetic: 107 us -> 12.6 us
  blocking collectives: 118 us -> 41 us
  loops' own time: 16.2 us -> 0 us
    all_to_all x21 -> x0, waiting for transfers between devices: 547 us -> none  [the longest x1 56.8 us: body(): lax.all_to_all(times_t(head_low, o_block).astype(jnp.bfloat16), 'hid', sp...]
    pallas_call x0 -> x12, Pallas kernels: none -> 480 us  [the longest x4 160 us: scatter_rows(): pl.pallas_call(scatter_kernel, out_shape=jax.ShapeDtypeStruct((rows, cols...]
    all_to_all x21 -> x0, starting transfers between devices: 169 us -> none  [the longest x1 15.3 us: body(): lax.all_to_all(times_t(hidden, down_block).astype(jnp.bfloat16), 'hid', s...]
    dot_general x87 -> x5, matrix products: 99 us -> 10.1 us  [the longest x1 3.32 us: fast_body(): up_lin = jnp.dot(second_rows, up_block, preferred_element_type=F32)]
    all_to_all x1 -> x0, blocking collectives: 76.2 us -> none  [body(): lax.all_to_all(fan_rows(second_low), 'hid', split_axis=0, concat_axis=0,...]
    convert_element_type x17 -> x0, local copies, waits for them, and re-layouts: 54 us -> none  [the longest x14 46.2 us: body(): q_back, f_back, i_back, o_back, gate_back, up_back, down_back = (lax.all_...]
    reduce_sum x18 -> x1, other arithmetic: 43.8 us -> 0.77 us  [doc_starts(): return jnp.sum(jnp.where(earlier, lengths[None, :], 0), axis=1)]
    broadcast_in_dim x21 -> x1, local copies, waits for them, and re-layouts: 35.8 us -> 0.07 us  [fast_body(): gap_row = lax.dynamic_slice_in_dim(gap_log, head_id * SPAN, SPAN)[None]]
  transfers between devices with their start and end apart: 23 -> 0, of which waited for: 18 -> 0; matrix products, arithmetic and copies ran while one was open for 31% -> 0% of each run, Pallas kernels for 0% -> 0%
where the time goes in v1:
time: 576 us; the launch traced here: 568 us
  Pallas kernels  480 us (83%)
  blocking collectives  41 us (7%)
  matrix products  30.4 us (5%)
  other arithmetic  12.6 us (2%)
    pallas_call x4, Pallas kernels, scatter_rows(): pl.pallas_call(scatter_kernel, out_shape=jax.ShapeDtypeStruct((rows, cols...  160 us
    pallas_call x4, Pallas kernels, gather_rows(): pl.pallas_call(gather_kernel, out_shape=jax.ShapeDtypeStruct((4, 2, 2) +...  149 us
    pallas_call x1, Pallas kernels, return_grads(): pl.pallas_call(functools.partial(grads_kernel, tiles), out_shape=[shape(m...  85.1 us
    pallas_call x1, Pallas kernels, fetch_weights(): pl.pallas_call(functools.partial(weights_kernel, tiles), out_shape=[shape...  76.3 us
    psum x1, blocking collectives, fast_body(): lax.psum((first_part, second_part, group_part[0], gap_full), ('seq', 'hid'))  41 us
    dot_general x5, matrix products, outer_sum(): lax.dot_general(left_mat, right_mat, (((0,), (0,)), ((), ())), preferred_...  12 us

profile of v1, /device:TPU:2, one launch (start us, length us, event | category | flops | bytes accessed | tf_op | source)
XLA Modules:
  0.0 567.5 jit_solution(5487036953039841532)
XLA Ops:
  3.5 1.1 fusion.8
  5.1 1.0 fusion.3.x_ref
  6.4 40.6 %shard_map.237 = bf16[4,2,2,48,2048]{4,3,2,1,0:T(8,128)(2,1)S(1)} custom-call(bf16[48,2048]{1,0:T(8,128)(2,1)S(1)} %fusion.3.x_ref), custom_call_target="tpu_custom_call" | custom-call | tf_op jit(solution)/shard_map/pallas_call | solution.py:523
  47.1 38.2 %shard_map.243 = bf16[4,2,2,48,2048]{4,3,2,1,0:T(8,128)(2,1)S(1)} custom-call(bf16[48,2048]{1,0:T(8,128)(2,1)S(1)} %bitcast.88), custom_call_target="tpu_custom_call" | custom-call | tf_op jit(solution)/shard_map/pallas_call | solution.py:523
  85.4 76.3 %shard_map.238 = (bf16[2048,384]{1,0:T(8,128)(2,1)S(1)}, bf16[2048,128]{1,0:T(8,128)(2,1)S(1)}, bf16[2048,384]{1,0:T(8,128)(2,1)}, bf16[2048,384]{1,0:T(8,128)(2,1)}, bf16[2048,384]{1,0:T(8,128)(2,1)}) custom-call(bf16[64,2048]{1,0:T(8,128)(2,1)S(1)} %copy-done.6, bf16[64,2048]{1,0:T(8,128)(2,1)S(1)} %copy-done.7, bf16[64,2048]{1,0:T(8,128)(2,1)S(1)} %copy-done.8, ...), custom_call_target="tpu_custom_call" | custom-call | tf_op jit(solution)/shard_map/pallas_call | solution.py:765
  161.7 1.8 fusion.16.lin_ref
  163.5 4.2 shard_map.239
  168.7 44.0 %shard_map.240 = f32[48,2048]{1,0:T(8,128)S(1)} custom-call(bf16[4,2,2,48,2048]{4,3,2,1,0:T(8,128)(2,1)S(1)} %bitcast.77), custom_call_target="tpu_custom_call" | custom-call | tf_op jit(solution)/shard_map/pallas_call | solution.py:603
  213.0 42.0 %shard_map.241 = bf16[4,2,2,48,2048]{4,3,2,1,0:T(8,128)(2,1)S(1)} custom-call(bf16[48,2048]{1,0:T(8,128)(2,1)S(1)} %multiply_convert_fusion.3.x_ref), custom_call_target="tpu_custom_call" | custom-call | tf_op jit(solution)/shard_map/pallas_call | solution.py:523
  255.0 3.3 fusion.18
  258.4 1.8 fusion.17
  260.2 2.2 multiply_convert_fusion
  262.4 3.0 fusion.pd
  265.5 3.0 convolution_convert_fusion.4.pu
  268.5 3.0 convolution_convert_fusion.5.pg
  271.5 1.8 convolution_convert_fusion.1
  273.4 36.5 %shard_map.242 = f32[48,2048]{1,0:T(8,128)S(1)} custom-call(bf16[4,2,2,48,2048]{4,3,2,1,0:T(8,128)(2,1)S(1)} %bitcast.86), custom_call_target="tpu_custom_call" | custom-call | tf_op jit(solution)/shard_map/pallas_call | solution.py:603
  309.9 1.8 fusion.19
  311.8 1.8 add_convert_fusion
  313.6 37.5 %shard_map.244 = f32[48,2048]{1,0:T(8,128)S(1)} custom-call(bf16[4,2,2,48,2048]{4,3,2,1,0:T(8,128)(2,1)S(1)} %bitcast.76), custom_call_target="tpu_custom_call" | custom-call | tf_op jit(solution)/shard_map/pallas_call | solution.py:603
  351.5 28.5 %shard_map.245 = bf16[4,2,2,48,2048]{4,3,2,1,0:T(8,128)(2,1)S(1)} custom-call(bf16[48,2048]{1,0:T(8,128)(2,1)S(1)} %fusion.15.x_ref), custom_call_target="tpu_custom_call" | custom-call | tf_op jit(solution)/shard_map/pallas_call | solution.py:523
  381.0 1.0 convolution_convert_fusion.7.po
  382.1 4.7 shard_map.246
  386.8 1.9 convolution_convert_fusion.6.pqfi
  388.7 85.1 %shard_map.248 = (bf16[64,2048]{1,0:T(8,128)(2,1)S(1)}, bf16[64,2048]{1,0:T(8,128)(2,1)S(1)}, bf16[64,2048]{1,0:T(8,128)(2,1)S(1)}, bf16[64,2048]{1,0:T(8,128)(2...) custom-call(bf16[2048,384]{1,0:T(8,128)(2,1)S(1)} %convolution_convert_fusion.6.pq, ...), custom_call_target="tpu_custom_call" | custom-call | tf_op jit(solution)/shard_map/pallas_call | solution.py:878
  477.2 1.2 convert_element_type.123
  478.4 1.2 convert_element_type.124
  479.6 1.2 convert_element_type.125
  480.8 1.8 convolution_convert_fusion
  482.6 42.2 %shard_map.247 = f32[48,2048]{1,0:T(8,128)S(1)} custom-call(bf16[4,2,2,48,2048]{4,3,2,1,0:T(8,128)(2,1)S(1)} %bitcast.87), custom_call_target="tpu_custom_call" | custom-call | tf_op jit(solution)/shard_map/pallas_call | solution.py:603
  525.1 1.0 fusion.7
  526.1 41.0 %all-reduce = (f32[2048]{0:T(1024)}, f32[128]{0:T(128)}, f32[2048]{0:T(1024)}, f32[2048]{0:T(1024)}) all-reduce(f32[2048]{0:T(1024)S(1)} %get-tuple-element.53, f32[128]{0:T(128)S(1)} %bitcast.91, f32[2048]{0:T(1024)S(1)} %multiply_bitcast_fusion, f32[2048]{0:T(1024)S(1)} %get-tuple-element.51), channel_id=1, replica_groups=mesh['seq'=2,'hid'=16] {'seq','hid'}, use_global_device_ids=true, to_apply=%region_8.9 | all-reduce | flops 6272 | bytes 50176 | tf_op jit(solution)/shard_map/psum | solution.py:1154
  (72 shorter events, 9.2 us)
Async XLA Ops:
  0.6 0.7 copy-start
  6.4 40.7 %copy-start.2 = (bf16[1,48,2048]{2,1,0:T(8,128)(2,1)S(1)}, bf16[1,48,2048]{2,1,0:T(8,128)(2,1)}, u32[]{:S(2)}) copy-start(bf16[1,48,2048]{2,1,0:T(8,128)(2,1)} %param.15) | copy-start | bytes 589828
  47.0 38.3 %copy-start.3 = (bf16[64,5632]{1,0:T(8,128)(2,1)S(1)}, bf16[64,5632]{1,0:T(8,128)(2,1)}, u32[]{:S(2)}) copy-start(bf16[64,5632]{1,0:T(8,128)(2,1)} %g.1) | copy-start | bytes 2162692
  47.0 38.3 %copy-start.4 = (bf16[64,5632]{1,0:T(8,128)(2,1)S(1)}, bf16[64,5632]{1,0:T(8,128)(2,1)}, u32[]{:S(2)}) copy-start(bf16[64,5632]{1,0:T(8,128)(2,1)} %u.1) | copy-start | bytes 2162692
  47.0 38.3 %copy-start.5 = (bf16[64,5632]{1,0:T(8,128)(2,1)S(1)}, bf16[64,5632]{1,0:T(8,128)(2,1)}, u32[]{:S(2)}) copy-start(bf16[64,5632]{1,0:T(8,128)(2,1)} %d.1) | copy-start | bytes 2162692
  47.0 38.3 %copy-start.6 = (bf16[64,2048]{1,0:T(8,128)(2,1)S(1)}, bf16[64,2048]{1,0:T(8,128)(2,1)}, u32[]{:S(2)}) copy-start(bf16[64,2048]{1,0:T(8,128)(2,1)} %q.1) | copy-start | bytes 786436
  47.1 38.3 %copy-start.7 = (bf16[64,2048]{1,0:T(8,128)(2,1)S(1)}, bf16[64,2048]{1,0:T(8,128)(2,1)}, u32[]{:S(2)}) copy-start(bf16[64,2048]{1,0:T(8,128)(2,1)} %f.1) | copy-start | bytes 786436
  47.1 38.3 %copy-start.8 = (bf16[64,2048]{1,0:T(8,128)(2,1)S(1)}, bf16[64,2048]{1,0:T(8,128)(2,1)}, u32[]{:S(2)}) copy-start(bf16[64,2048]{1,0:T(8,128)(2,1)} %i.1) | copy-start | bytes 786436
  47.1 38.3 %copy-start.9 = (bf16[64,2048]{1,0:T(8,128)(2,1)S(1)}, bf16[64,2048]{1,0:T(8,128)(2,1)}, u32[]{:S(2)}) copy-start(bf16[64,2048]{1,0:T(8,128)(2,1)} %o.1) | copy-start | bytes 786436
  161.7 1.8 copy-start.10
  168.7 44.0 %copy-start.11 = (bf16[1,48,2048]{2,1,0:T(8,128)(2,1)S(1)}, bf16[1,48,2048]{2,1,0:T(8,128)(2,1)}, u32[]{:S(2)}) copy-start(bf16[1,48,2048]{2,1,0:T(8,128)(2,1)} %param.14) | copy-start | bytes 589828
  168.7 44.2 %copy-start.19 = (f32[2048]{0:T(1024)S(1)}, f32[2048]{0:T(1024)}, u32[]{:S(2)}) copy-start(f32[2048]{0:T(1024)} %param.24) | copy-start | bytes 24580
  255.0 3.3 copy-start.13
  258.4 1.8 copy-start.21
  262.4 3.0 copy-start.17
  262.4 6.1 %copy-start.15 = (bf16[768,384]{1,0:T(8,128)(2,1)}, bf16[768,384]{1,0:T(8,128)(2,1)S(1)}, u32[]{:S(2)}) copy-start(bf16[768,384]{1,0:T(8,128)(2,1)S(1)} %get-tuple-element.62) | copy-start | bytes 1769476
  273.3 36.6 %copy-start.14 = (bf16[2048,384]{1,0:T(8,128)(2,1)S(1)}, bf16[2048,384]{1,0:T(8,128)(2,1)}, u32[]{:S(2)}) copy-start(bf16[2048,384]{1,0:T(8,128)(2,1)} %get-tuple-element.35) | copy-start | bytes 4718596
  273.3 36.6 %copy-start.16 = (bf16[768,384]{1,0:T(8,128)(2,1)S(1)}, bf16[768,384]{1,0:T(8,128)(2,1)}, u32[]{:S(2)}) copy-start(bf16[768,384]{1,0:T(8,128)(2,1)} %copy-done.15) | copy-start | bytes 1769476
  309.9 1.8 copy-start.12
  309.9 1.8 copy-start.18
  482.6 42.3 %copy-start.20 = (f32[2048]{0:T(1024)S(1)}, f32[2048]{0:T(1024)}, u32[]{:S(2)}) copy-start(f32[2048]{0:T(1024)} %param.17) | copy-start | bytes 24580
  482.6 84.5 %copy-start.1 = (f32[2048]{0:T(1024)S(1)}, f32[2048]{0:T(1024)}, u32[]{:S(2)}) copy-start(f32[2048]{0:T(1024)} %param.23) | copy-start | bytes 24580

commit v2 on v0

--- a/solution.py
+++ b/solution.py
@@ -1,6 +1,10 @@
+import functools
+
 import jax
 import jax.numpy as jnp
 from jax import lax
+from jax.experimental import pallas as pl
+from jax.experimental.pallas import tpu as pltpu
 from jax.sharding import PartitionSpec as P
 
 H = 16
@@ -27,15 +31,32 @@
     return (jax.nn.silu(q_part), key_gate, jnp.log1p(-key_gate))
 
 
+def doc_starts(lengths):
+    count = lengths.shape[0]
+    earlier = lax.broadcasted_iota(jnp.int32, (count, count), 0) > lax.broadcasted_iota(
+        jnp.int32, (count, count), 1
+    )
+    return jnp.sum(jnp.where(earlier, lengths[None, :], 0), axis=1)
+
+
+def running_sum(rows):
+    extent = rows.shape[-2]
+    lower = (
+        lax.broadcasted_iota(jnp.int32, (extent, extent), 0)
+        >= lax.broadcasted_iota(jnp.int32, (extent, extent), 1)
+    ).astype(jnp.float32)
+    return jnp.einsum("ts,...sk->...tk", lower, rows, precision=HIGH_PRECISION)
+
+
 def doc_ids(lengths, positions):
-    starts = jnp.cumsum(lengths) - lengths
+    starts = doc_starts(lengths)
     covered = (starts[None, :] <= positions[:, None]).astype(jnp.int32)
     return jnp.sum(covered, axis=1) - 1
 
 
 def span_step(memory_state, pieces):
     queries, key_gate, value_rows, log_decay, documents, before = pieces
-    cumulative = jnp.cumsum(log_decay, axis=1)
+    cumulative = running_sum(log_decay)
     query_decayed = queries * jnp.exp(cumulative)
     k_grown = key_gate * jnp.exp(-cumulative)
     extent = documents.shape[0]
@@ -138,7 +159,7 @@
     )
 
 
-def body(
+def wide_body(
     inputs,
     cotangent,
     lengths,
@@ -226,7 +247,7 @@
     i_lin = jnp.dot(first_rows, i_block, preferred_element_type=jnp.float32)
     gap_part = lax.dynamic_slice_in_dim(gap_log, head_id * head_width, head_width)
     queries, key_gate, log_decay = gates(q_lin, f_lin, gap_part)
-    cumulative = jnp.cumsum(log_decay, axis=0)
+    cumulative = running_sum(log_decay)
     last_cum = cumulative[-1]
     tail_key_rows = (
         jnp.exp(last_cum[None, :] - cumulative)
@@ -384,6 +405,1012 @@
     )
 
 
+F32 = jnp.float32
+BF = jnp.bfloat16
+MESH = pl.DeviceIdType.MESH
+DMA = pltpu.SemaphoreType.DMA
+VMEM = pltpu.VMEM
+PIECES = 3
+PARTS = 4
+CUTS = PIECES * PARTS
+AHEAD = (4, 4, 4, 4)
+PACE = (4, 5)
+VSPEC = pl.BlockSpec(memory_space=pltpu.VMEM)
+ASPEC = pl.BlockSpec(memory_space=pl.ANY)
+SSPEC = pl.BlockSpec(memory_space=pltpu.SMEM)
+
+
+def place():
+    h = lax.axis_index("hid")
+    return h, h // 4, lax.rem(h // 2, 2), lax.rem(h, 2)
+
+
+def partners():
+    h, z, y, x = place()
+    column = [lax.rem(z + k, 4) * 4 + lax.rem(h, 4) for k in (1, 2, 3)]
+    return column, h + 2 - 4 * y, h + 1 - 2 * x
+
+
+def greet(chips, core=False):
+    gate = pltpu.get_barrier_semaphore()
+    for chip in chips:
+        pl.semaphore_signal(gate, inc=1, device_id={"hid": chip}, device_id_type=MESH)
+    if core:
+        other = 1 - lax.axis_index("seq")
+        pl.semaphore_signal(gate, inc=1, device_id={"seq": other}, device_id_type=MESH)
+    pl.semaphore_wait(gate, len(chips) + int(core))
+
+
+def to_chip(src, dst, send, recv, chip):
+    return pltpu.make_async_remote_copy(
+        src_ref=src,
+        dst_ref=dst,
+        send_sem=send,
+        recv_sem=recv,
+        device_id={"hid": chip},
+        device_id_type=MESH,
+    )
+
+
+def to_core(src, dst, send, recv):
+    return pltpu.make_async_remote_copy(
+        src_ref=src,
+        dst_ref=dst,
+        send_sem=send,
+        recv_sem=recv,
+        device_id={"seq": 1 - lax.axis_index("seq")},
+        device_id_type=MESH,
+    )
+
+
+def comm_params(collective_id):
+    return pltpu.CompilerParams(
+        collective_id=collective_id, has_side_effects=True, vmem_limit_bytes=56 << 20
+    )
+
+
+class Cuts:
+    def cut(self, c):
+        i, j = c // PARTS, c % PARTS
+        rows, cols = self.ref.shape[3] // PIECES, self.ref.shape[4] // PARTS
+        return pl.ds(i * rows, rows), pl.ds(j * cols, cols), j % 2
+
+
+class Gather(Cuts):
+    def __init__(self, ref, sems):
+        self.ref, self.sems = ref, sems
+        self.one, self.two, self.three = {}, {}, {}
+
+    def start(self, c):
+        h, z, y, x = place()
+        column, py, px = partners()
+        a, b, j = self.cut(c)
+        ref = self.ref.at[z, y, x, a, b]
+        for k in range(3):
+            self.one[c, k] = to_chip(
+                ref, ref, self.sems[0].at[c, k], self.sems[1].at[c, k], column[k]
+            )
+            self.one[c, k].start()
+
+    def second(self, c):
+        h, z, y, x = place()
+        column, py, px = partners()
+        a, b, j = self.cut(c)
+        for k in range(3):
+            self.one[c, k].wait_recv()
+        ref = self.ref.at[:, y, x, a, b]
+        self.two[c] = to_chip(ref, ref, self.sems[2].at[c], self.sems[3].at[c], py if j else px)
+        self.two[c].start()
+
+    def third(self, c):
+        h, z, y, x = place()
+        column, py, px = partners()
+        a, b, j = self.cut(c)
+        self.two[c].wait_recv()
+        ref = self.ref.at[:, :, x, a, b] if j else self.ref.at[:, y, :, a, b]
+        self.three[c] = to_chip(ref, ref, self.sems[4].at[c], self.sems[5].at[c], px if j else py)
+        self.three[c].start()
+
+    def finish(self):
+        for c in self.three:
+            self.three[c].wait_recv()
+        for c in self.three:
+            for k in range(3):
+                self.one[c, k].wait_send()
+            self.two[c].wait_send()
+            self.three[c].wait_send()
+
+
+def gather_sems():
+    n = CUTS
+    return [DMA((n, 3)), DMA((n, 3)), DMA((n,)), DMA((n,)), DMA((n,)), DMA((n,))]
+
+
+class Scatter(Cuts):
+    def __init__(self, ref, scratch):
+        self.ref, self.bufs, self.sems = ref, scratch[:5], scratch[5:]
+        self.one, self.two, self.three = {}, {}, {}
+
+    def start(self, c):
+        h, z, y, x = place()
+        column, py, px = partners()
+        a, b, j = self.cut(c)
+        src = self.ref.at[:, :, 1 - x, a, b] if j else self.ref.at[:, 1 - y, :, a, b]
+        self.one[c] = to_chip(
+            src, self.bufs[0].at[c], self.sems[0].at[c], self.sems[1].at[c], px if j else py
+        )
+        self.one[c].start()
+
+    def second(self, c):
+        h, z, y, x = place()
+        column, py, px = partners()
+        b1, t1, b2 = self.bufs[:3]
+        a, b, j = self.cut(c)
+        q = y if j else x
+        self.one[c].wait_recv()
+        theirs = self.ref[:, 1 - q, x, a, b] if j else self.ref[:, y, 1 - q, a, b]
+        b1[c, :, 1 - q] = (theirs.astype(F32) + b1[c, :, 1 - q].astype(F32)).astype(BF)
+        self.two[c] = to_chip(
+            b1.at[c, :, 1 - q], b2.at[c], self.sems[2].at[c], self.sems[3].at[c], py if j else px
+        )
+        self.two[c].start()
+        mine = self.ref[:, q, x, a, b] if j else self.ref[:, y, q, a, b]
+        t1[c] = mine.astype(F32) + b1[c, :, q].astype(F32)
+
+    def third(self, c):
+        h, z, y, x = place()
+        column, py, px = partners()
+        b1, t1, b2, t2, b3 = self.bufs
+        self.two[c].wait_recv()
+        t2[c] = t1[c] + b2[c].astype(F32)
+        b2[c] = t2[c].astype(BF)
+        for k in range(3):
+            self.three[c, k] = to_chip(
+                b2.at[c, lax.rem(z + k + 1, 4)],
+                b3.at[c, k],
+                self.sems[4].at[c, k],
+                self.sems[5].at[c, k],
+                column[k],
+            )
+            self.three[c, k].start()
+
+    def last(self, c):
+        h, z, y, x = place()
+        b3, t2 = self.bufs[4], self.bufs[3]
+        for k in range(3):
+            self.three[c, k].wait_recv()
+        return t2[c, z] + b3[c, 0].astype(F32) + b3[c, 1].astype(F32) + b3[c, 2].astype(F32)
+
+    def finish(self):
+        for c in self.one:
+            self.one[c].wait_send()
+            self.two[c].wait_send()
+            for k in range(3):
+                self.three[c, k].wait_send()
+
+
+def scatter_scratch(rows, cols):
+    n, r, w = CUTS, rows // PIECES, cols // PARTS
+    return [
+        VMEM((n, 4, 2, r, w), BF),
+        VMEM((n, 4, r, w), F32),
+        VMEM((n, 4, r, w), BF),
+        VMEM((n, 4, r, w), F32),
+        VMEM((n, 3, r, w), BF),
+        DMA((n,)),
+        DMA((n,)),
+        DMA((n,)),
+        DMA((n,)),
+        DMA((n, 3)),
+        DMA((n, 3)),
+    ]
+
+
+def all_chips():
+    h = lax.axis_index("hid")
+    return [lax.rem(h + k, H) for k in range(1, H)]
+
+
+class Queue:
+    def __init__(self, jobs):
+        self.jobs = list(jobs)
+
+    def run(self, number):
+        for job in self.jobs[:number]:
+            job()
+        self.jobs = self.jobs[number:]
+
+
+def unit_span(tiles, h):
+    first = (tiles * h) // H
+    return first, (tiles * (h + 1)) // H - first
+
+
+def lanes(tile, count):
+    return pl.ds(pl.multiple_of(tile * 128, 128), count * 128)
+
+
+class Bulk:
+    def __init__(self, items, tiles, depth, sems):
+        self.items, self.tiles, self.depth = items, tiles, depth
+        self.ss, self.rs, self.ls, self.xs, self.xr = sems
+        self.least = tiles // H
+
+    def sized(self, n, chip, act):
+        if not self.items[n][3]:
+            act(chip, 1)
+            return
+        first, count = unit_span(self.tiles, chip)
+        if self.tiles % H == 0:
+            act(first, self.least)
+            return
+        for number in (self.least, self.least + 1):
+            pl.when(count == number)(functools.partial(act, first, number))
+
+    def ours(self, view):
+        half = H * self.depth
+        return pl.ds(pl.multiple_of(view * half, half), half)
+
+    def row(self, core, chip):
+        return pl.ds(pl.multiple_of((core * H + chip) * self.depth, self.depth), self.depth)
+
+
+class Fetch(Bulk):
+    def copy(self, n, k, chip, first, count):
+        h, b = lax.axis_index("hid"), lax.axis_index("seq")
+        src, dst, at, _ = self.items[n]
+        return to_chip(
+            src.at[:, lanes(first, count)],
+            dst.at[self.row(b, h), lanes(at, count)],
+            self.ss.at[n, k],
+            self.rs.at[n, k],
+            chip,
+        )
+
+    def own(self, n, first, count):
+        h, b = lax.axis_index("hid"), lax.axis_index("seq")
+        src, dst, at, _ = self.items[n]
+        return pltpu.make_async_copy(
+            src.at[:, lanes(first, count)], dst.at[self.row(b, h), lanes(at, count)], self.ls.at[n]
+        )
+
+    def job(self, n, k):
+        def run():
+            chip = lax.rem(lax.axis_index("hid") + k, H)
+            self.sized(
+                n, chip, lambda first, count: self.copy(n, k, chip, first, count).start()
+            )
+
+        return run
+
+    def jobs(self):
+        return [self.job(n, k) for n in range(len(self.items)) for k in range(1, H)]
+
+    def start_own(self):
+        h = lax.axis_index("hid")
+        for n, (_, dst, _, split) in enumerate(self.items):
+            self.sized(n, h, lambda first, count: self.own(n, first, count).start())
+            if split and self.tiles % H:
+
+                @pl.when(unit_span(self.tiles, h)[1] == self.least)
+                def _():
+                    dst[:, self.least * 128 :] = jnp.zeros((dst.shape[0], 128), BF)
+
+    def swap(self, n, tile, count, slot):
+        b = lax.axis_index("seq")
+        view = self.items[n][1].at[self.ours(b), lanes(tile, count)]
+        return to_core(view, view, self.xs.at[n, slot], self.xr.at[n, slot])
+
+    def each_swap(self, n, act):
+        at, split = self.items[n][2:]
+        act(self.swap(n, at, self.least if split else 1, 0))
+        if split and self.tiles % H:
+
+            @pl.when(unit_span(self.tiles, lax.axis_index("hid"))[1] > self.least)
+            def _():
+                act(self.swap(n, self.least, 1, 1))
+
+    def arrive(self, n):
+        h = lax.axis_index("hid")
+        self.sized(n, h, lambda first, count: self.own(n, first, count).wait())
+        for k in range(1, H):
+            self.sized(
+                n, h, lambda first, count: self.copy(n, k, h, first, count).wait_recv()
+            )
+        self.each_swap(n, lambda copy: copy.start())
+
+    def finish(self):
+        for n in range(len(self.items)):
+            self.each_swap(n, lambda copy: copy.wait())
+            for k in range(1, H):
+                chip = lax.rem(lax.axis_index("hid") + k, H)
+                self.sized(
+                    n, chip, lambda first, count: self.copy(n, k, chip, first, count).wait_send()
+                )
+
+
+class Return(Bulk):
+    def __init__(self, items, parts, tiles, depth, sems):
+        super().__init__(items, tiles, depth, sems)
+        self.parts = parts
+
+    def swap(self, p):
+        part, total, _ = self.parts[p]
+        return to_core(
+            part.at[self.ours(1 - lax.axis_index("seq"))], total, self.xs.at[p, 0], self.xr.at[p, 0]
+        )
+
+    def start_swaps(self):
+        for p in range(len(self.parts)):
+            self.swap(p).start()
+
+    def add(self, p):
+        def run():
+            part, total, _ = self.parts[p]
+            b = lax.axis_index("seq")
+            self.swap(p).wait()
+            half, step = total.shape[0], 128
+
+            @pl.loop(0, half // step)
+            def _(t):
+                at = pl.ds(pl.multiple_of(t * step, step), step)
+                own = pl.ds(pl.multiple_of(b * half + t * step, step), step)
+                total[at] = (total[at].astype(F32) + part[own].astype(F32)).astype(BF)
+
+            for n in self.parts[p][2]:
+                h = lax.axis_index("hid")
+                self.sized(n, h, lambda first, count: self.own(n, first, count).start())
+
+        return run
+
+    def copy(self, n, k, chip, first, count):
+        dst, src, at, _ = self.items[n]
+        return to_chip(
+            src.at[self.row(0, chip), lanes(at, count)],
+            dst.at[:, lanes(first, count)],
+            self.ss.at[n, k],
+            self.rs.at[n, k],
+            chip,
+        )
+
+    def own(self, n, first, count):
+        dst, src, at, _ = self.items[n]
+        return pltpu.make_async_copy(
+            src.at[self.row(0, lax.axis_index("hid")), lanes(at, count)],
+            dst.at[:, lanes(first, count)],
+            self.ls.at[n],
+        )
+
+    def job(self, n, k):
+        def run():
+            h = lax.axis_index("hid")
+            chip = lax.rem(h + k, H)
+            self.sized(n, h, lambda first, count: self.copy(n, k, chip, first, count).start())
+
+        return run
+
+    def jobs(self):
+        made = []
+        for p, (_, _, ns) in enumerate(self.parts):
+            made.append(self.add(p))
+            made += [self.job(n, k) for n in ns for k in range(1, H)]
+        return made
+
+    def finish(self):
+        h = lax.axis_index("hid")
+        for n in range(len(self.items)):
+            self.sized(n, h, lambda first, count: self.own(n, first, count).wait())
+            for k in range(1, H):
+                chip, source = lax.rem(h + k, H), lax.rem(h + H - k, H)
+                self.sized(
+                    n, source, lambda first, count: self.copy(n, k, chip, first, count).wait_recv()
+                )
+                self.sized(
+                    n, h, lambda first, count: self.copy(n, k, chip, first, count).wait_send()
+                )
+
+
+def bulk_sems(n):
+    return [DMA((n, H)), DMA((n, H)), DMA((n,)), DMA((n, 2)), DMA((n, 2))]
+
+
+def split_refs(refs, *counts):
+    groups, at = [], 0
+    for count in counts:
+        groups.append(refs[at : at + count])
+        at += count
+    assert at == len(refs)
+    return groups
+
+
+def row_norm(rows):
+    return lax.rsqrt(jnp.mean(rows * rows, axis=-1, keepdims=True) + EPS)
+
+
+def open_kernel(tiles, *refs):
+    (x_ref, c_ref, *weights), (first, cot, wqfi, wo, wg, wu, wd), s1, s2, bulk, (ls,) = split_refs(
+        refs, 9, 7, 6, 6, 5, 1
+    )
+    q, f, i, o, g, u, d = weights
+    h, z, y, x = place()
+    greet(all_chips(), core=True)
+    own = [
+        pltpu.make_async_copy(src, dst.at[z, y, x], ls.at[n])
+        for n, (src, dst) in enumerate(((x_ref, first), (c_ref, cot)))
+    ]
+    for copy in own:
+        copy.start()
+    fetch = Fetch(
+        [
+            (q, wqfi, 0, False),
+            (f, wqfi, 1, False),
+            (i, wqfi, 2, False),
+            (o, wo, 0, False),
+            (g, wg, 0, True),
+            (u, wu, 0, True),
+            (d, wd, 0, True),
+        ],
+        tiles,
+        q.shape[0],
+        bulk,
+    )
+    for copy in own:
+        copy.wait()
+    queue = Queue(fetch.jobs())
+    gathers = [Gather(first, s1), Gather(cot, s2)]
+    cuts = [(g, c) for g in gathers for c in range(CUTS)]
+    for g, c in cuts[: AHEAD[0]]:
+        g.start(c)
+    queue.run(PACE[0])
+    fetch.start_own()
+    n = len(cuts)
+    for t in range(n + PARTS):
+        if t < n:
+            cuts[t][0].second(cuts[t][1])
+        if t + AHEAD[0] < n:
+            g, c = cuts[t + AHEAD[0]]
+            g.start(c)
+        if t >= PARTS:
+            cuts[t - PARTS][0].third(cuts[t - PARTS][1])
+        queue.run(PACE[0])
+    queue.run(len(queue.jobs))
+    for k in range(len(weights)):
+        fetch.arrive(k)
+    for g in gathers:
+        g.finish()
+    fetch.finish()
+
+
+def open_segment(first_low, cot_low, weights, collective_id):
+    depth, units = weights[-1].shape
+    tiles = units // 128
+    wide = -(-tiles // H) * 128
+    shape = lambda cols: jax.ShapeDtypeStruct((2 * H * depth, cols), BF)
+    rows = jax.ShapeDtypeStruct((4, 2, 2) + first_low.shape, BF)
+    first, cot, *blocks = pl.pallas_call(
+        functools.partial(open_kernel, tiles),
+        out_shape=[rows, rows] + [shape(cols) for cols in (384, 128, wide, wide, wide)],
+        in_specs=[VSPEC] * 2 + [ASPEC] * 7,
+        out_specs=[VSPEC] * 7,
+        scratch_shapes=gather_sems() + gather_sems() + bulk_sems(7) + [DMA((2,))],
+        compiler_params=comm_params(collective_id),
+    )(first_low, cot_low, *weights)
+    flat = lambda rows: rows.reshape(-1, rows.shape[-1])
+    return flat(first), flat(cot), *blocks
+
+
+def turn_steps(scatter, gather, ahead, rows_done):
+    n, lag, held = CUTS, PARTS, []
+    for c in range(min(ahead, n)):
+        scatter.start(c)
+    for t in range(n + 5 * lag):
+        if t < n:
+            scatter.second(t)
+            if t + ahead < n:
+                scatter.start(t + ahead)
+        if 0 <= t - lag // 2 < n:
+            scatter.third(t - lag // 2)
+        c = t - lag - lag // 2
+        if 0 <= c < n:
+            held.append(scatter.last(c))
+            if len(held) == PARTS:
+                rows_done(c // PARTS, jnp.concatenate(held, axis=1))
+                held = []
+                for k in range(c + 1 - PARTS, c + 1):
+                    gather.start(k)
+        c -= lag + PARTS - 1
+        if 0 <= c < n:
+            gather.second(c)
+        if 0 <= c - lag < n:
+            gather.third(c - lag)
+    scatter.finish()
+    gather.finish()
+
+
+def forward_kernel(p_ref, x_ref, gain_ref, middle, second, *scratch):
+    h, z, y, x = place()
+    column, py, px = partners()
+    greet(column + [py, px])
+    s1, s2 = split_refs(scratch, 11, 6)
+    scatter, gather = Scatter(p_ref, s1), Gather(second, s2)
+    size = x_ref.shape[0] // PIECES
+
+    def rows_done(i, total):
+        at = pl.ds(i * size, size)
+        rows = x_ref[at] + total
+        middle[at] = rows
+        second[z, y, x, at] = (rows * row_norm(rows) * gain_ref[...]).astype(BF)
+
+    turn_steps(scatter, gather, AHEAD[1], rows_done)
+
+
+def forward_segment(part, entries, gain, collective_id):
+    rows, cols = entries.shape
+    middle, second = pl.pallas_call(
+        forward_kernel,
+        out_shape=[
+            jax.ShapeDtypeStruct((rows, cols), F32),
+            jax.ShapeDtypeStruct((4, 2, 2, rows, cols), BF),
+        ],
+        in_specs=[VSPEC] * 3,
+        out_specs=[VSPEC] * 2,
+        scratch_shapes=scatter_scratch(rows, cols) + gather_sems(),
+        compiler_params=comm_params(collective_id),
+    )(part.reshape(4, 2, 2, rows, cols), entries, gain[None])
+    return middle, second.reshape(-1, cols)
+
+
+def norm_back(rows, grad, gain):
+    factor = row_norm(rows)
+    normal = rows * factor
+    scaled = grad * gain
+    back = factor * (scaled - normal * jnp.mean(scaled * normal, axis=-1, keepdims=True))
+    return back, jnp.sum(grad * normal, axis=0, keepdims=True)
+
+
+def backward_kernel(p_ref, m_ref, c_ref, gain_ref, grad, mix, part, *scratch):
+    h, z, y, x = place()
+    column, py, px = partners()
+    greet(column + [py, px])
+    s1, s2 = split_refs(scratch, 11, 6)
+    scatter, gather = Scatter(p_ref, s1), Gather(mix, s2)
+    size = m_ref.shape[0] // PIECES
+
+    def rows_done(i, total):
+        at = pl.ds(i * size, size)
+        back, gains = norm_back(m_ref[at], total, gain_ref[...])
+        part[...] = gains if i == 0 else part[...] + gains
+        rows = c_ref[at].astype(F32) + back
+        grad[at] = rows
+        mix[z, y, x, at] = rows.astype(BF)
+
+    turn_steps(scatter, gather, AHEAD[2], rows_done)
+
+
+def backward_segment(part, middle, cot_low, gain, collective_id):
+    rows, cols = middle.shape
+    grad, mix, gains = pl.pallas_call(
+        backward_kernel,
+        out_shape=[
+            jax.ShapeDtypeStruct((rows, cols), F32),
+            jax.ShapeDtypeStruct((4, 2, 2, rows, cols), BF),
+            jax.ShapeDtypeStruct((1, cols), F32),
+        ],
+        in_specs=[VSPEC] * 4,
+        out_specs=[VSPEC] * 3,
+        scratch_shapes=scatter_scratch(rows, cols) + gather_sems(),
+        compiler_params=comm_params(collective_id),
+    )(part.reshape(4, 2, 2, rows, cols), middle, cot_low, gain[None])
+    return grad, mix.reshape(-1, cols), gains
+
+
+def close_kernel(tiles, *refs):
+    (
+        (p_ref, l_ref, x_ref, mg_ref, m_ref, gain_ref, vec_ref, pqfi, po, pg, pu, pd),
+        (in_grad, out, totals, q, f, i, o, g, u, d),
+        s1,
+        s2,
+        (tqfi, to, tg, tu, td),
+        (mine, theirs, chips, vs, vr, ws, wr),
+        bulk,
+    ) = split_refs(refs, 12, 10, 11, 11, 5, 7, 5)
+    h, z, y, x = place()
+    greet(all_chips(), core=True)
+    giver = Return(
+        [
+            (d, td, 0, True),
+            (g, tg, 0, True),
+            (u, tu, 0, True),
+            (o, to, 0, False),
+            (q, tqfi, 0, False),
+            (f, tqfi, 1, False),
+            (i, tqfi, 2, False),
+        ],
+        [(pd, td, (0,)), (pg, tg, (1,)), (pu, tu, (2,)), (po, to, (3,)), (pqfi, tqfi, (4, 5, 6))],
+        tiles,
+        q.shape[0],
+        bulk,
+    )
+    first, glu = Scatter(p_ref, s1), Scatter(l_ref, s2)
+    size = x_ref.shape[0] // PIECES
+    queue = Queue(giver.jobs())
+    cuts = [(s, c) for s in (first, glu) for c in range(CUTS)]
+    giver.start_swaps()
+    for s, c in cuts[: AHEAD[3]]:
+        s.start(c)
+    held, sent = [], {}
+    total, lag = len(cuts), PARTS
+    for t in range(total + lag + lag // 2):
+        if t < total:
+            cuts[t][0].second(cuts[t][1])
+            if t + AHEAD[3] < total:
+                s, c = cuts[t + AHEAD[3]]
+                s.start(c)
+        if 0 <= t - lag // 2 < total:
+            s, c = cuts[t - lag // 2]
+            s.third(c)
+        if 0 <= t - lag - lag // 2 < total:
+            s, c = cuts[t - lag - lag // 2]
+            held.append(s.last(c))
+            if len(held) == PARTS:
+                at = pl.ds(c // PARTS * size, size)
+                rows = jnp.concatenate(held, axis=1)
+                held = []
+                if s is first:
+                    back, gains = norm_back(x_ref[at], rows, gain_ref[...])
+                    in_grad[at] = mg_ref[at] + back
+                    if c < PARTS:
+                        mine[...] = vec_ref[...]
+                    mine[0:16] = mine[0:16] + gains.reshape(16, 128)
+                    if c == CUTS - 1:
+                        swap = to_core(mine, theirs, vs, vr)
+                        swap.start()
+                else:
+                    out[at] = (m_ref[at] + rows).astype(BF)
+        if t == CUTS + 2 * lag:
+            swap.wait()
+            chips[h] = mine[...] + theirs[...]
+            for k in range(1, H):
+                sent[k] = to_chip(
+                    chips.at[h], chips.at[h], ws.at[k], wr.at[k], lax.rem(h + k, H)
+                )
+                sent[k].start()
+        queue.run(PACE[1])
+    queue.run(len(queue.jobs))
+    for k in range(1, H):
+        sent[k].wait()
+    acc = chips[0, 0:40]
+    for chip in range(1, H):
+        acc = acc + chips[chip, 0:40]
+    totals[0:40] = acc
+    for chip in range(H):
+        totals[40 + chip : 41 + chip] = chips[chip, 40:41]
+    first.finish()
+    glu.finish()
+    giver.finish()
+
+
+def close_segment(
+    part, glu, entries, middle_grad, middle, gain, vector, grads, units, collective_id
+):
+    rows, cols = entries.shape
+    depth = grads[0].shape[0] // (2 * H)
+    back = lambda width: jax.ShapeDtypeStruct((depth, width), BF)
+    wide = (4, 2, 2, rows, cols)
+    return pl.pallas_call(
+        functools.partial(close_kernel, units // 128),
+        out_shape=[
+            jax.ShapeDtypeStruct((rows, cols), F32),
+            jax.ShapeDtypeStruct((rows, cols), BF),
+            jax.ShapeDtypeStruct((56, 128), F32),
+        ]
+        + [back(cols)] * 4
+        + [back(units)] * 3,
+        in_specs=[VSPEC] * 12,
+        out_specs=[VSPEC] * 10,
+        scratch_shapes=scatter_scratch(rows, cols)
+        + scatter_scratch(rows, cols)
+        + [VMEM((p.shape[0] // 2, p.shape[1]), BF) for p in grads]
+        + [VMEM((48, 128), F32), VMEM((48, 128), F32), VMEM((H, 48, 128), F32)]
+        + [DMA, DMA, DMA((H,)), DMA((H,))]
+        + bulk_sems(7),
+        compiler_params=comm_params(collective_id),
+    )(
+        part.reshape(wide),
+        glu.reshape(wide),
+        entries,
+        middle_grad,
+        middle,
+        gain[None],
+        vector,
+        *grads,
+    )
+
+
+def mm(left, right, at_left, at_right):
+    return lax.dot_general(
+        left.astype(BF),
+        right.astype(BF),
+        (((at_left,), (at_right,)), ((), ())),
+        preferred_element_type=F32,
+    )
+
+
+def tri_sum(rows, reverse=False):
+    r = lax.broadcasted_iota(jnp.int32, (SPAN, SPAN), 0)
+    c = lax.broadcasted_iota(jnp.int32, (SPAN, SPAN), 1)
+    picked = jnp.where((r <= c) if reverse else (r >= c), 1.0, 0.0).astype(BF)
+    high = rows.astype(BF)
+    rest = rows - high.astype(F32)
+    middle = rest.astype(BF)
+    low = rest - middle.astype(F32)
+    return mm(picked, high, 1, 0) + mm(picked, middle, 1, 0) + mm(picked, low, 1, 0)
+
+
+def span_gates(lin_ref, gap_ref, at):
+    q_lin, f_lin, values = lin_ref[at, 0:128], lin_ref[at, 128:256], lin_ref[at, 256:384]
+    s = jax.nn.sigmoid(q_lin)
+    key = jnp.exp(gap_ref[...]) * jax.nn.sigmoid(-f_lin)
+    return q_lin, f_lin, values, s, key
+
+
+def span_masks(dcol_ref, drow_ref, marks_ref, c, at):
+    r = lax.broadcasted_iota(jnp.int32, (SPAN, SPAN), 0)
+    k = lax.broadcasted_iota(jnp.int32, (SPAN, SPAN), 1)
+    dcol, drow = dcol_ref[at], drow_ref[c : c + 1]
+    before, end = marks_ref[0, c], marks_ref[1, c]
+    same = jnp.where(jnp.logical_and(dcol == drow, r >= k), 1.0, 0.0)
+    carried = jnp.where(dcol == before, 1.0, 0.0)
+    keep = jnp.where(dcol == end, 1.0, 0.0)
+    whole = jnp.where(end == before, 1.0, 0.0)
+    return same, carried, keep, whole
+
+
+def spans(extent):
+    return [(c, pl.ds(c * SPAN, SPAN)) for c in range(extent // SPAN)]
+
+
+def mix_kernel(
+    lin_ref, gap_ref, gain_ref, dcol_ref, drow_ref, marks_ref,
+    mixed_ref, states_ref, head_ref, cum_ref, out_ref, in_ref, send, recv,
+):
+    greet([], core=True)
+    extent = lin_ref.shape[0]
+    steps = spans(extent)
+    state = jnp.zeros((SPAN, SPAN), F32)
+    for c, at in steps:
+        q_lin, f_lin, values, s, key = span_gates(lin_ref, gap_ref, at)
+        same, carried, keep, whole = span_masks(dcol_ref, drow_ref, marks_ref, c, at)
+        cum = tri_sum(jnp.log1p(-key))
+        cum_ref[at] = cum
+        end = cum[SPAN - 1 : SPAN]
+        fresh = mm(values, jnp.exp(end - cum) * key * keep, 0, 0)
+        states_ref[c] = fresh
+        state = state * (jnp.exp(end) * whole) + fresh
+    out_ref[...] = state
+    copy = to_core(out_ref, in_ref, send, recv)
+    copy.start()
+    copy.wait()
+    state = in_ref[...] * lax.axis_index("seq").astype(F32)
+    for c, at in steps:
+        q_lin, f_lin, values, s, key = span_gates(lin_ref, gap_ref, at)
+        same, carried, keep, whole = span_masks(dcol_ref, drow_ref, marks_ref, c, at)
+        cum = cum_ref[at]
+        end = cum[SPAN - 1 : SPAN]
+        fresh = states_ref[c]
+        states_ref[c] = state
+        decayed = q_lin * s * jnp.exp(cum)
+        scores = mm(decayed, key * jnp.exp(-cum), 1, 1) * same
+        mixed = mm(scores, values, 1, 0) + carried * mm(decayed, state, 1, 1)
+        mixed_ref[at] = mixed
+        factor = lax.rsqrt(jnp.mean(mixed * mixed, axis=-1, keepdims=True) + EPS)
+        head_ref[at] = (mixed * factor * gain_ref[...]).astype(BF)
+        state = state * (jnp.exp(end) * whole) + fresh
+
+
+def mix_forward(lin, gap_row, gain_row, dcol, drow, marks, collective_id):
+    extent = lin.shape[0]
+    tile = jax.ShapeDtypeStruct((extent, SPAN), F32)
+    return pl.pallas_call(
+        mix_kernel,
+        out_shape=[
+            tile,
+            jax.ShapeDtypeStruct((extent // SPAN, SPAN, SPAN), F32),
+            jax.ShapeDtypeStruct((extent, SPAN), BF),
+            tile,
+        ],
+        in_specs=[VSPEC] * 5 + [SSPEC],
+        out_specs=[VSPEC] * 4,
+        scratch_shapes=[VMEM((SPAN, SPAN), F32), VMEM((SPAN, SPAN), F32), DMA, DMA],
+        compiler_params=comm_params(collective_id),
+    )(lin, gap_row, gain_row, dcol, drow, marks)
+
+
+def unmix_kernel(
+    lin_ref, gap_ref, gain_ref, dcol_ref, drow_ref, marks_ref, mixed_ref, states_ref, cum_ref, dhead_ref,
+    dlin_ref, gapg_ref, groupg_ref, do_ref, back_ref, out_ref, in_ref, send, recv,
+):
+    greet([], core=True)
+    extent = lin_ref.shape[0]
+    steps = spans(extent)
+    group = jnp.zeros((1, SPAN), F32)
+    adjoint = jnp.zeros((SPAN, SPAN), F32)
+    for c, at in reversed(steps):
+        mixed, dy = mixed_ref[at], dhead_ref[at]
+        factor = lax.rsqrt(jnp.mean(mixed * mixed, axis=-1, keepdims=True) + EPS)
+        normal = mixed * factor
+        group = group + jnp.sum(dy * normal, axis=0, keepdims=True)
+        scaled = dy * gain_ref[...]
+        d_mixed = factor * (scaled - normal * jnp.mean(scaled * normal, axis=-1, keepdims=True))
+        do_ref[at] = d_mixed
+        q_lin, f_lin, values, s, key = span_gates(lin_ref, gap_ref, at)
+        same, carried, keep, whole = span_masks(dcol_ref, drow_ref, marks_ref, c, at)
+        cum = cum_ref[at]
+        back = mm(d_mixed, carried * (q_lin * s * jnp.exp(cum)), 0, 0)
+        back_ref[c] = back
+        adjoint = adjoint * (jnp.exp(cum[SPAN - 1 : SPAN]) * whole) + back
+    groupg_ref[...] = group
+    out_ref[...] = adjoint
+    copy = to_core(out_ref, in_ref, send, recv)
+    copy.start()
+    copy.wait()
+    adjoint = in_ref[...] * (1 - lax.axis_index("seq")).astype(F32)
+    gap = jnp.zeros((1, SPAN), F32)
+    for c, at in reversed(steps):
+        q_lin, f_lin, values, s, key = span_gates(lin_ref, gap_ref, at)
+        same, carried, keep, whole = span_masks(dcol_ref, drow_ref, marks_ref, c, at)
+        cum, d_mixed, state = cum_ref[at], do_ref[at], states_ref[c]
+        grow, shrink = jnp.exp(-cum), jnp.exp(cum)
+        end = cum[SPAN - 1 : SPAN]
+        decayed, grown = q_lin * s * shrink, key * grow
+        rest = jnp.exp(end - cum) * keep
+        tail, through = rest * key, jnp.exp(end) * whole
+        scores = mm(decayed, grown, 1, 1) * same
+        d_scores = mm(d_mixed, values, 1, 1) * same
+        d_values = mm(scores, d_mixed, 0, 0) + mm(tail, adjoint, 1, 1)
+        d_decayed = mm(d_scores, grown, 1, 0) + carried * mm(d_mixed, state, 1, 0)
+        d_grown = mm(d_scores, decayed, 0, 0)
+        d_tail = mm(values, adjoint, 1, 0)
+        held = tail * d_tail
+        d_cum = decayed * d_decayed - grown * d_grown - held
+        d_end = jnp.sum(held, axis=0, keepdims=True) + through * jnp.sum(
+            state * adjoint, axis=0, keepdims=True
+        )
+        d_log = tri_sum(d_cum, reverse=True) + d_end
+        d_key = d_grown * grow + d_tail * rest - d_log / (1.0 - key)
+        scaled = d_key * key
+        gap = gap + jnp.sum(scaled, axis=0, keepdims=True)
+        dlin_ref[at, 0:128] = (d_decayed * shrink * s * (1.0 + q_lin * (1.0 - s))).astype(BF)
+        dlin_ref[at, 128:256] = (-scaled * jax.nn.sigmoid(f_lin)).astype(BF)
+        dlin_ref[at, 256:384] = d_values.astype(BF)
+        adjoint = adjoint * through + back_ref[c]
+    gapg_ref[...] = gap
+
+
+def mix_backward(lin, gap_row, gain_row, dcol, drow, marks, mixed, states, cum, d_head, collective_id):
+    extent = lin.shape[0]
+    row = jax.ShapeDtypeStruct((1, SPAN), F32)
+    return pl.pallas_call(
+        unmix_kernel,
+        out_shape=[jax.ShapeDtypeStruct(lin.shape, BF), row, row],
+        in_specs=[VSPEC] * 5 + [SSPEC] + [VSPEC] * 4,
+        out_specs=[VSPEC] * 3,
+        scratch_shapes=[
+            VMEM((extent, SPAN), F32),
+            VMEM((extent // SPAN, SPAN, SPAN), F32),
+            VMEM((SPAN, SPAN), F32),
+            VMEM((SPAN, SPAN), F32),
+            DMA,
+            DMA,
+        ],
+        compiler_params=comm_params(collective_id),
+    )(lin, gap_row, gain_row, dcol, drow, marks, mixed, states, cum, d_head)
+
+
+def fast_body(
+    inputs,
+    cotangent,
+    lengths,
+    first_gain,
+    q_weight,
+    f_weight,
+    i_weight,
+    o_weight,
+    group_gain,
+    gap_log,
+    second_gain,
+    gate_weight,
+    up_weight,
+    down_weight,
+):
+    rows, model = inputs.shape[1:]
+    units = gate_weight.shape[1]
+    head_id, block_id = lax.axis_index("hid"), lax.axis_index("seq")
+    block_len = H * rows
+    entries = inputs[0].astype(F32)
+    cot_low = cotangent[0]
+    positions = block_id * block_len + lax.iota(jnp.int32, block_len)
+    documents = doc_ids(lengths, positions)
+    before = doc_ids(lengths, jnp.reshape(block_id * block_len - 1, (1,)))
+    drow = documents.reshape(block_len // SPAN, SPAN)
+    ends = drow[:, -1]
+    marks = jnp.stack([jnp.concatenate([before, ends[:-1]]), ends])
+    gap_row = lax.dynamic_slice_in_dim(gap_log, head_id * SPAN, SPAN)[None]
+    gain_row = group_gain[None]
+    aids = (gap_row, gain_row, documents[:, None], drow, marks)
+
+    first_low = normed(entries, first_gain).astype(BF)
+    first_rows, cot_rows, qfi_block, o_block, gate_block, up_block, down_block = open_segment(
+        first_low,
+        cot_low,
+        (q_weight, f_weight, i_weight, o_weight, gate_weight, up_weight, down_weight),
+        1,
+    )
+    lin = jnp.dot(first_rows, qfi_block, preferred_element_type=F32)
+    mixed, states, head_low, cum = mix_forward(lin, *aids, 2)
+    middle, second_rows = forward_segment(
+        times_t(head_low, o_block).astype(BF), entries, second_gain, 3
+    )
+    gate_lin = jnp.dot(second_rows, gate_block, preferred_element_type=F32)
+    up_lin = jnp.dot(second_rows, up_block, preferred_element_type=F32)
+    gate_sig = jax.nn.sigmoid(gate_lin)
+    hidden = (gate_lin * gate_sig * up_lin).astype(BF)
+    hidden_grad = jnp.dot(cot_rows, down_block, preferred_element_type=F32)
+    gate_low = (hidden_grad * up_lin * gate_sig * (1.0 + gate_lin * (1.0 - gate_sig))).astype(BF)
+    up_low = (hidden_grad * gate_lin * gate_sig).astype(BF)
+    second_sum = (times_t(gate_low, gate_block) + times_t(up_low, up_block)).astype(BF)
+    middle_grad, mix_rows, second_part = backward_segment(
+        second_sum, middle, cot_low, second_gain, 4
+    )
+    d_head = jnp.dot(mix_rows, o_block, preferred_element_type=F32)
+    d_lin, gap_part, group_part = mix_backward(lin, *aids, mixed, states, cum, d_head, 5)
+    vector = jnp.concatenate(
+        [
+            jnp.zeros((16, 128), F32),
+            second_part.reshape(16, 128),
+            group_part,
+            jnp.zeros((7, 128), F32),
+            gap_part,
+            jnp.zeros((7, 128), F32),
+        ]
+    )
+    input_grad, output, totals, q_grad, f_grad, i_grad, o_grad, gate_grad, up_grad, down_grad = (
+        close_segment(
+            times_t(d_lin, qfi_block).astype(BF),
+            times_t(hidden, down_block).astype(BF),
+            entries,
+            middle_grad,
+            middle,
+            first_gain,
+            vector,
+            (
+                outer_sum(first_rows, d_lin).astype(BF),
+                outer_sum(mix_rows, head_low).astype(BF),
+                outer_sum(second_rows, gate_low).astype(BF),
+                outer_sum(second_rows, up_low).astype(BF),
+                outer_sum(cot_rows, hidden).astype(BF),
+            ),
+            units,
+            6,
+        )
+    )
+    return (
+        output[None],
+        input_grad[None],
+        totals[0:16].reshape(model),
+        q_grad.astype(F32),
+        f_grad.astype(F32),
+        i_grad.astype(F32),
+        o_grad.astype(F32),
+        totals[32],
+        totals[40:56].reshape(model),
+        totals[16:32].reshape(model),
+        gate_grad.astype(F32),
+        up_grad.astype(F32),
+        down_grad.astype(F32),
+    )
+
+
 def solution(mesh):
     placed = (
         P("seq", "hid", None),
@@ -401,6 +1428,7 @@
         P(("seq", "hid"), None),
         P(("seq", "hid"), None),
     )
+    body = fast_body if mesh.shape["hid"] == H else wide_body
     return jax.shard_map(
         body,
         mesh=mesh,

time: 1310 us -> 504 us (0.38)
  waiting for transfers between devices: 547 us -> 0 us
  Pallas kernels: 0 us -> 420 us
  starting transfers between devices: 172 us -> 0 us
  local copies, waits for them, and re-layouts: 180 us -> 9.24 us
  blocking collectives: 118 us -> 0 us
  matrix products: 148 us -> 48.2 us
  other arithmetic: 107 us -> 15.5 us
  loops' own time: 16.2 us -> 0 us
    all_to_all x21 -> x0, waiting for transfers between devices: 547 us -> none  [the longest x1 56.8 us: body(): lax.all_to_all(times_t(head_low, o_block).astype(jnp.bfloat16), 'hid', sp...]
    pallas_call x0 -> x6, Pallas kernels: none -> 420 us  [the longest x1 139 us: close_segment(): pl.pallas_call(functools.partial(close_kernel, units // 128), out_shape=[...]
    all_to_all x21 -> x0, starting transfers between devices: 169 us -> none  [the longest x1 15.3 us: body(): lax.all_to_all(times_t(hidden, down_block).astype(jnp.bfloat16), 'hid', s...]
    dot_general x87 -> x5, matrix products: 99 us -> 17.1 us  [the longest x1 5.3 us: fast_body(): lin = jnp.dot(first_rows, qfi_block, preferred_element_type=F32)]
    all_to_all x1 -> x0, blocking collectives: 76.2 us -> none  [body(): lax.all_to_all(fan_rows(second_low), 'hid', split_axis=0, concat_axis=0,...]
    convert_element_type x17 -> x0, local copies, waits for them, and re-layouts: 54 us -> none  [the longest x14 46.2 us: body(): q_back, f_back, i_back, o_back, gate_back, up_back, down_back = (lax.all_...]
    reduce_sum x20 -> x1, other arithmetic: 44.8 us -> 0.77 us  [doc_starts(): return jnp.sum(jnp.where(earlier, lengths[None, :], 0), axis=1)]
    psum x1 -> x0, blocking collectives: 41.8 us -> none  [body(): lax.psum((first_part, second_part, group_part, gap_full), ('seq', 'hid'))]
  transfers between devices with their start and end apart: 23 -> 0, of which waited for: 18 -> 0; matrix products, arithmetic and copies ran while one was open for 31% -> 0% of each run, Pallas kernels for 0% -> 0%
where the time goes in v2:
time: 504 us; the launch traced here: 495 us
  Pallas kernels  420 us (83%)
  matrix products  48.2 us (10%)
  other arithmetic  15.5 us (3%)
  local copies, waits for them, and re-layouts  9.24 us (2%)
    pallas_call x1, Pallas kernels, close_segment(): pl.pallas_call(functools.partial(close_kernel, units // 128), out_shape=[...  139 us
    pallas_call x1, Pallas kernels, open_segment(): pl.pallas_call(functools.partial(open_kernel, tiles), out_shape=[rows, ro...  118 us
    pallas_call x1, Pallas kernels, forward_segment(): pl.pallas_call(forward_kernel, out_shape=[jax.ShapeDtypeStruct((rows, col...  77.1 us
    pallas_call x1, Pallas kernels, backward_segment(): pl.pallas_call(backward_kernel, out_shape=[jax.ShapeDtypeStruct((rows, co...  72.9 us
    dot_general x5, matrix products, times_t(): lax.dot_general(left_mat, right_mat, (((1,), (1,)), ((), ())), preferred_...  16 us
    dot_general x5, matrix products, outer_sum(): lax.dot_general(left_mat, right_mat, (((0,), (0,)), ((), ())), preferred_...  15.2 us

profile of v2, /device:TPU:2, one launch (start us, length us, event | category | flops | bytes accessed | tf_op | source)
XLA Modules:
  0.0 494.6 jit_solution(6063215916730283619)
XLA Ops:
  4.0 1.1 multiply_reduce_fusion
  6.2 1.7 multiply_convert_fusion.3.refs_0_
  8.9 1.7 bitcast_convert_fusion.x_ref.refs_2_
  10.6 118.3 %shard_map.237 = (bf16[4,2,2,48,2048]{4,3,2,1,0:T(8,128)(2,1)}, bf16[4,2,2,48,2048]{4,3,2,1,0:T(8,128)(2,1)}, bf16[2048,384]{1,0:T(8,128)(2,1)}, bf16[2048,128]{...) custom-call(bf16[48,2048]{1,0:T(8,128)(2,1)} %multiply_convert_fusion.3.refs_0_, ...), custom_call_target="tpu_custom_call" | custom-call | tf_op jit(solution)/shard_map/pallas_call | solution.py:890
  128.9 5.3 %fusion.2.lin_ref = f32[768,384]{1,0:T(8,128)} fusion(bf16[768,2048]{1,0:T(8,128)(2,1)} %bitcast.83, bf16[2048,384]{1,0:T(8,128)(2,1)} %get-tuple-element.43), kind=kOutput, calls=%fused_computation.34 | convolution fusion | flops 1207959552 | bytes 5898240 | tf_op jit(solution)/shard_map/dot_general | solution.py:1349
  134.2 1.8 fusion.3
  136.0 5.8 %shard_map.238 = (f32[768,128]{1,0:T(8,128)}, f32[6,128,128]{2,1,0:T(8,128)}, bf16[768,128]{1,0:T(8,128)(2,1)}, f32[768,128]{1,0:T(8,128)}) custom-call(f32[768,384]{1,0:T(8,128)} %fusion.2.lin_ref, f32[1,128]{1,0:T(1,128)} %dynamic-slice_bitcast_fusion.gap_ref, f32[1,128]{1,0:T(1,128)} %bitcast.81, s32[768,1]{1,0:T(8,128)} %sub.26.dcol_ref, ...), custom_call_target="tpu_custom_call" | custom-call | tf_op jit(solution)/shard_map/pallas_call | solution.py:1214
  141.8 3.6 convolution_convert_fusion.2
  145.5 77.1 %shard_map.239 = (f32[48,2048]{1,0:T(8,128)}, bf16[4,2,2,48,2048]{4,3,2,1,0:T(8,128)(2,1)}) custom-call(bf16[4,2,2,48,2048]{4,3,2,1,0:T(8,128)(2,1)} %bitcast.69, f32[48,2048]{1,0:T(8,128)} %bitcast_convert_fusion.x_ref.refs_2_, f32[1,2048]{1,0:T(1,128)} %bitcast.77), custom_call_target="tpu_custom_call" | custom-call | tf_op jit(solution)/shard_map/pallas_call | solution.py:949
  222.6 4.0 fusion.4
  226.6 2.2 multiply_convert_fusion
  228.9 3.1 convolution_convert_fusion.3.refs_11_
  231.9 3.5 convolution_convert_fusion
  235.4 3.0 convolution_convert_fusion.5.refs_9_
  238.4 3.0 convolution_convert_fusion.4.refs_10_
  241.5 1.8 fusion.5
  243.3 3.5 add_convert_fusion
  246.8 72.9 %shard_map.240 = (f32[48,2048]{1,0:T(8,128)}, bf16[4,2,2,48,2048]{4,3,2,1,0:T(8,128)(2,1)}, f32[1,2048]{1,0:T(1,128)}) custom-call(bf16[4,2,2,48,2048]{4,3,2,1,0:T(8,128)(2,1)} %bitcast.68, f32[48,2048]{1,0:T(8,128)} %get-tuple-element.54.m_ref.refs_4_, bf16[48,2048]{1,0:T(8,128)(2,1)} %bitcast.73, f32[1,2048]{1,0:T(1,128)} %bitcast.78), custom_call_target="tpu_custom_call" | custom-call | tf_op jit(solution)/shard_map/pallas_call | solution.py:992
  319.7 3.8 fusion.6.dhead_ref
  323.5 1.8 convolution_convert_fusion.7.refs_8_
  325.3 6.9 %shard_map.241 = (bf16[768,384]{1,0:T(8,128)(2,1)}, f32[1,128]{1,0:T(1,128)}, f32[1,128]{1,0:T(1,128)}) custom-call(f32[768,384]{1,0:T(8,128)} %fusion.2.lin_ref, f32[1,128]{1,0:T(1,128)} %dynamic-slice_bitcast_fusion.gap_ref, f32[1,128]{1,0:T(1,128)} %bitcast.82, s32[768,1]{1,0:T(8,128)} %sub.26.dcol_ref, s32[6,128]{1,0:T(8,128)} %copy-done.14, ...), custom_call_target="tpu_custom_call" | custom-call | tf_op jit(solution)/shard_map/pallas_call | solution.py:1293
  332.3 4.2 convolution_convert_fusion.6.refs_7_
  336.6 2.4 concatenate.7.refs_6_
  339.0 3.5 convolution_convert_fusion.1
  342.5 138.6 %shard_map.242 = (f32[48,2048]{1,0:T(8,128)}, bf16[48,2048]{1,0:T(8,128)(2,1)}, f32[56,128]{1,0:T(8,128)}, bf16[64,2048]{1,0:T(8,128)(2,1)}, bf16[64,2048]{1,0:T...) custom-call(bf16[4,2,2,48,2048]{4,3,2,1,0:T(8,128)(2,1)} %bitcast.71, ...), custom_call_target="tpu_custom_call" | custom-call | tf_op jit(solution)/shard_map/pallas_call | solution.py:1100
  481.1 1.2 slice_bitcast_fusion.3
  482.4 1.3 slice_bitcast_fusion
  483.7 1.8 convert_element_type.91
  485.6 1.8 convert_element_type.92
  489.0 1.2 convert_element_type.95
  490.2 1.2 convert_element_type.96
  491.6 1.2 convert_element_type.97
  (66 shorter events, 8.1 us)
Async XLA Ops:
  0.6 0.7 copy-start
  5.2 123.7 %copy-start.14 = (s32[6,128]{1,0:T(8,128)}, s32[6,128]{1,0:T(8,128)S(1)}, u32[]{:S(2)}) copy-start(s32[6,128]{1,0:T(8,128)S(1)} %get-tuple-element.77.drow_ref) | copy-start | bytes 9220
  128.9 5.3 %copy-start.19 = (bf16[4,2,2,48,2048]{4,3,2,1,0:T(8,128)(2,1)S(1)}, bf16[4,2,2,48,2048]{4,3,2,1,0:T(8,128)(2,1)}, u32[]{:S(2)}) copy-start(bf16[4,2,2,48,2048]{4,3,2,1,0:T(8,128)(2,1)} %get-tuple-element.47) | copy-start | bytes 9437188
  128.9 5.3 %copy-start.22 = (bf16[2048,384]{1,0:T(8,128)(2,1)S(1)}, bf16[2048,384]{1,0:T(8,128)(2,1)}, u32[]{:S(2)}) copy-start(bf16[2048,384]{1,0:T(8,128)(2,1)} %get-tuple-element.48) | copy-start | bytes 4718596
  136.0 5.8 %copy-start.3 = (bf16[2048,128]{1,0:T(8,128)(2,1)S(1)}, bf16[2048,128]{1,0:T(8,128)(2,1)}, u32[]{:S(2)}) copy-start(bf16[2048,128]{1,0:T(8,128)(2,1)} %get-tuple-element.50) | copy-start | bytes 1572868
  145.5 77.1 %copy-start.5 = (bf16[2048,384]{1,0:T(8,128)(2,1)S(1)}, bf16[2048,384]{1,0:T(8,128)(2,1)}, u32[]{:S(2)}) copy-start(bf16[2048,384]{1,0:T(8,128)(2,1)} %get-tuple-element.53) | copy-start | bytes 4718596
  222.6 4.0 copy-start.4
  222.6 4.0 copy-start.20
  319.7 3.8 copy-start.2
  319.7 3.8 copy-start.6
  325.3 6.9 %copy-start.18 = (bf16[4,2,2,48,2048]{4,3,2,1,0:T(8,128)(2,1)S(1)}, bf16[4,2,2,48,2048]{4,3,2,1,0:T(8,128)(2,1)}, u32[]{:S(2)}) copy-start(bf16[4,2,2,48,2048]{4,3,2,1,0:T(8,128)(2,1)} %get-tuple-element.42) | copy-start | bytes 9437188
  332.3 4.3 copy-start.15
  332.3 4.3 copy-start.16
  332.3 4.3 copy-start.17
  332.3 6.7 %copy-start.21 = (bf16[2048,384]{1,0:T(8,128)(2,1)S(1)}, bf16[2048,384]{1,0:T(8,128)(2,1)}, u32[]{:S(2)}) copy-start(bf16[2048,384]{1,0:T(8,128)(2,1)} %get-tuple-element.43) | copy-start | bytes 4718596
  332.3 6.7 %copy-start.23 = (bf16[768,384]{1,0:T(8,128)(2,1)S(1)}, bf16[768,384]{1,0:T(8,128)(2,1)}, u32[]{:S(2)}) copy-start(bf16[768,384]{1,0:T(8,128)(2,1)} %get-tuple-element.56) | copy-start | bytes 1769476
  481.1 6.2 %copy-start.12 = (bf16[64,2048]{1,0:T(8,128)(2,1)S(1)}, bf16[64,2048]{1,0:T(8,128)(2,1)}, u32[]{:S(2)}) copy-start(bf16[64,2048]{1,0:T(8,128)(2,1)} %get-tuple-element.66) | copy-start | bytes 786436
  481.1 7.1 %copy-start.11 = (bf16[64,2048]{1,0:T(8,128)(2,1)S(1)}, bf16[64,2048]{1,0:T(8,128)(2,1)}, u32[]{:S(2)}) copy-start(bf16[64,2048]{1,0:T(8,128)(2,1)} %get-tuple-element.67) | copy-start | bytes 786436
  483.7 5.3 %copy-start.9 = (bf16[64,5632]{1,0:T(8,128)(2,1)S(1)}, bf16[64,5632]{1,0:T(8,128)(2,1)}, u32[]{:S(2)}) copy-start(bf16[64,5632]{1,0:T(8,128)(2,1)} %get-tuple-element.68) | copy-start | bytes 2162692
  488.2 2.0 copy-start.8
  490.2 1.4 copy-start.7
  490.2 4.0 copy-start.1
  491.6 1.2 copy-start.13
  491.6 1.9 copy-start.10
